TPU v7x, 32 devices: a whole 2x2x4 slice. The times are simulated.
32 devices in a mesh: dp: 16 (over z, y, x), tensor: 2 (over core).
Axes of the slice: x: 2, y: 2, z: 4, core: 2. Of those that a mesh axis runs over, the one named last changes fastest.
Arguments:
- block_input: bfloat16 [3136, 512], P('dp'), may hold values from -6 to 6
- ln1_gain: float32 [512], replicated, may hold values from 0.1 to 1.9
- ln1_bias: float32 [512], replicated, may hold values from -3 to 3
- w_qkv: bfloat16 [3, 512, 512], P(None, None, 'tensor'), may hold values from -0.25 to 0.25
- qv_bias: float32 [2, 512], P(None, 'tensor'), may hold values from -3 to 3
- bias_table: float32 [169, 16], P(None, 'tensor'), may hold values from -4 to 4
- w_proj: bfloat16 [512, 512], P('tensor'), may hold values from -1 to 1
- proj_bias: float32 [512], replicated, may hold values from -3 to 3
- ln2_gain: float32 [512], replicated, may hold values from 0.1 to 1.9
- ln2_bias: float32 [512], replicated, may hold values from -3 to 3
- w_fc1: bfloat16 [512, 2048], P(None, 'tensor'), may hold values from -0.25 to 0.25
- fc1_bias: float32 [2048], P('tensor'), may hold values from -3 to 3
- w_fc2: bfloat16 [2048, 512], P('tensor'), may hold values from -0.1875 to 0.1875
- fc2_bias: float32 [512], replicated, may hold values from -3 to 3
- region_ids: int32 [4, 49], replicated, may hold values from 0 to 3
- rel_index: int32 [49, 49], replicated, may hold values from 0 to 168
- cotangent: bfloat16 [3136, 512], P('dp'), may hold values from -6 to 6
Outputs:
- block_output: float32 [3136, 512], P('dp')
- dx: float32 [3136, 512], P('dp')
- g_ln1_gain: float32 [512], replicated
- g_ln1_bias: float32 [512], replicated
- g_qkv: float32 [3, 512, 512], P(None, None, 'tensor')
- g_qv_bias: float32 [2, 512], P(None, 'tensor')
- g_table: float32 [169, 16], P(None, 'tensor')
- g_proj: float32 [512, 512], P('tensor')
- g_proj_bias: float32 [512], replicated
- g_ln2_gain: float32 [512], replicated
- g_ln2_bias: float32 [512], replicated
- g_fc1: float32 [512, 2048], P(None, 'tensor')
- g_fc1_bias: float32 [2048], P('tensor')
- g_fc2: float32 [2048, 512], P('tensor')
- g_fc2_bias: float32 [512], replicated
All inputs are finite; a program needn't handle non-finite values.
Results may differ from a plain program's by a relative error of at most 0.012.
Values sent between devices are 32-bit elements; how exact they have to be, the bound alone decides.
No kernel may reach another device: no remote copies, remote signals or barrier semaphores. Data moves between devices by JAX's collectives and lax.ppermute only.
A program may use at most 64 MiB of HBM per device.

v0:
```python
import jax
import jax.numpy as jnp
from jax import lax
from jax.sharding import PartitionSpec as P

SIDE = 14
WIN = 7
SHIFT = 3
NWIN = 4
WTOK = 49
TABLE = 169


def layer_stats(values, gain, bias):
    mean = jnp.mean(values, -1, keepdims=True)
    centred = values - mean
    var = jnp.mean(centred * centred, -1, keepdims=True)
    rstd = lax.rsqrt(var + 1e-05)
    nhat = centred * rstd
    return (nhat * gain + bias, nhat, rstd)


def layer_back(dout, nhat, rstd, gain):
    dnorm = dout * gain
    return rstd * (
        dnorm
        - jnp.mean(dnorm, -1, keepdims=True)
        - nhat * jnp.mean(dnorm * nhat, -1, keepdims=True)
    )


def to_windows(values, nimg):
    width = values.shape[-1]
    per = SIDE // WIN
    grid = values.reshape(nimg, SIDE, SIDE, width)
    grid = jnp.roll(grid, (-SHIFT, -SHIFT), (1, 2))
    grid = grid.reshape(nimg, per, WIN, per, WIN, width).transpose(0, 1, 3, 2, 4, 5)
    return grid.reshape(-1, width)


def from_windows(values, nimg):
    width = values.shape[-1]
    per = SIDE // WIN
    grid = values.reshape(nimg, per, per, WIN, WIN, width).transpose(0, 1, 3, 2, 4, 5)
    grid = grid.reshape(nimg, SIDE, SIDE, width)
    grid = jnp.roll(grid, (SHIFT, SHIFT), (1, 2))
    return grid.reshape(-1, width)


def gelu_value(u):
    return 0.5 * u * (1.0 + lax.erf(u * 0.7071067811865476))


def gelu_slope(u):
    return (
        0.5 * (1.0 + lax.erf(u * 0.7071067811865476))
        + u * jnp.exp(-0.5 * u * u) * 0.3989422804014327
    )


def inner(left, right):
    return lax.dot_general(
        left, right, (((0,), (0,)), ((), ())), preferred_element_type=jnp.float32
    )


def outer(left, right):
    return lax.dot_general(
        left, right, (((1,), (1,)), ((), ())), preferred_element_type=jnp.float32
    )


def mixed(form, left, right):
    return jnp.einsum(form, left, right, preferred_element_type=jnp.float32)


def body(
    block_input,
    ln1_gain,
    ln1_bias,
    w_qkv,
    qv_bias,
    bias_table,
    w_proj,
    proj_bias,
    ln2_gain,
    ln2_bias,
    w_fc1,
    fc1_bias,
    w_fc2,
    fc2_bias,
    region_ids,
    rel_index,
    cotangent,
):
    nimg = block_input.shape[0] // (SIDE * SIDE)
    heads = bias_table.shape[1]
    local_width = w_qkv.shape[2]
    hdim = local_width // heads
    scale = hdim ** (-0.5)
    shape5 = (nimg, NWIN, WTOK, heads, hdim)
    onehot = (rel_index.reshape(-1)[:, None] == lax.iota(jnp.int32, TABLE)[None, :]).astype(
        jnp.float32
    )
    bias = jnp.dot(onehot, bias_table, precision=lax.Precision.HIGHEST).T.reshape(heads, WTOK, WTOK)
    same = region_ids[:, :, None] == region_ids[:, None, :]
    mask = jnp.where(same, jnp.float32(0.0), jnp.float32(-100.0))
    xf = block_input.astype(jnp.float32)
    anorm, nhat1, rstd1 = layer_stats(xf, ln1_gain, ln1_bias)
    aw = to_windows(anorm.astype(jnp.bfloat16), nimg)
    query = (
        (jnp.dot(aw, w_qkv[0], preferred_element_type=jnp.float32) + qv_bias[0]) * scale
    ).astype(jnp.bfloat16)
    keys = jnp.dot(aw, w_qkv[1], preferred_element_type=jnp.float32).astype(jnp.bfloat16)
    values = (jnp.dot(aw, w_qkv[2], preferred_element_type=jnp.float32) + qv_bias[1]).astype(
        jnp.bfloat16
    )
    q5 = query.reshape(shape5)
    k5 = keys.reshape(shape5)
    v5 = values.reshape(shape5)
    scores = mixed("nwihd,nwjhd->nwhij", q5, k5) + bias[None, None] + mask[None, :, None]
    expo = jnp.exp(scores)
    total = jnp.sum(expo, -1, keepdims=True)
    probs = expo / total
    lse = jnp.log(total)
    attn5 = mixed("nwhij,nwjhd->nwihd", probs.astype(jnp.bfloat16), v5).astype(jnp.bfloat16)
    attn_flat = attn5.reshape(-1, local_width)
    projected = lax.psum(jnp.dot(attn_flat, w_proj, preferred_element_type=jnp.float32), "tensor")
    hres = xf + from_windows(projected, nimg) + proj_bias
    cnorm, nhat2, rstd2 = layer_stats(hres, ln2_gain, ln2_bias)
    cb = cnorm.astype(jnp.bfloat16)
    upre = jnp.dot(cb, w_fc1, preferred_element_type=jnp.float32) + fc1_bias
    zact = gelu_value(upre).astype(jnp.bfloat16)
    mlp_out = lax.psum(jnp.dot(zact, w_fc2, preferred_element_type=jnp.float32), "tensor")
    block_output = hres + mlp_out + fc2_bias
    gf = cotangent.astype(jnp.float32)
    g_fc2_bias = jnp.sum(gf, 0)
    g_fc2 = inner(zact, cotangent)
    du = outer(cotangent, w_fc2) * gelu_slope(upre)
    g_fc1_bias = jnp.sum(du, 0)
    dub = du.astype(jnp.bfloat16)
    g_fc1 = inner(cb, dub)
    dcn = lax.psum(outer(dub, w_fc1), "tensor")
    g_ln2_gain = jnp.sum(dcn * nhat2, 0)
    g_ln2_bias = jnp.sum(dcn, 0)
    dh = gf + layer_back(dcn, nhat2, rstd2, ln2_gain)
    g_proj_bias = jnp.sum(dh, 0)
    dhw = to_windows(dh, nimg).astype(jnp.bfloat16)
    g_proj = inner(attn_flat, dhw)
    dout = outer(dhw, w_proj).astype(jnp.bfloat16)
    d5 = dout.reshape(shape5)
    scores = mixed("nwihd,nwjhd->nwhij", q5, k5) + bias[None, None] + mask[None, :, None]
    probs = jnp.exp(scores - lse)
    pb = probs.astype(jnp.bfloat16)
    dprob = mixed("nwihd,nwjhd->nwhij", d5, v5)
    delta = jnp.sum(d5.astype(jnp.float32) * attn5.astype(jnp.float32), -1).transpose(0, 1, 3, 2)[
        ..., None
    ]
    dscore = probs * (dprob - delta)
    dv = mixed("nwhij,nwihd->nwjhd", pb, d5).reshape(-1, local_width)
    dbias = jnp.sum(dscore, (0, 1)).reshape(heads, WTOK * WTOK)
    g_table = lax.dot_general(
        onehot, dbias, (((0,), (1,)), ((), ())), precision=lax.Precision.HIGHEST
    )
    dsb = dscore.astype(jnp.bfloat16)
    dq = (mixed("nwhij,nwjhd->nwihd", dsb, k5) * scale).reshape(-1, local_width)
    dk = mixed("nwhij,nwihd->nwjhd", dsb, q5).reshape(-1, local_width)
    g_qv_bias = jnp.stack([jnp.sum(dq, 0), jnp.sum(dv, 0)])
    dqb = dq.astype(jnp.bfloat16)
    dkb = dk.astype(jnp.bfloat16)
    dvb = dv.astype(jnp.bfloat16)
    g_qkv = jnp.stack([inner(aw, dqb), inner(aw, dkb), inner(aw, dvb)])
    daw = outer(dqb, w_qkv[0]) + outer(dkb, w_qkv[1]) + outer(dvb, w_qkv[2])
    dan = lax.psum(from_windows(daw, nimg), "tensor")
    g_ln1_gain = jnp.sum(dan * nhat1, 0)
    g_ln1_bias = jnp.sum(dan, 0)
    dx = dh + layer_back(dan, nhat1, rstd1, ln1_gain)
    (
        g_ln1_gain,
        g_ln1_bias,
        g_qkv,
        g_qv_bias,
        g_table,
        g_proj,
        g_proj_bias,
        g_ln2_gain,
        g_ln2_bias,
        g_fc1,
        g_fc1_bias,
        g_fc2,
        g_fc2_bias,
    ) = lax.psum(
        (
            g_ln1_gain,
            g_ln1_bias,
            g_qkv,
            g_qv_bias,
            g_table,
            g_proj,
            g_proj_bias,
            g_ln2_gain,
            g_ln2_bias,
            g_fc1,
            g_fc1_bias,
            g_fc2,
            g_fc2_bias,
        ),
        "dp",
    )
    return (
        block_output,
        dx,
        g_ln1_gain,
        g_ln1_bias,
        g_qkv,
        g_qv_bias,
        g_table,
        g_proj,
        g_proj_bias,
        g_ln2_gain,
        g_ln2_bias,
        g_fc1,
        g_fc1_bias,
        g_fc2,
        g_fc2_bias,
    )


def solution(mesh):
    return jax.shard_map(
        body,
        mesh=mesh,
        in_specs=(
            P("dp", None),
            P(),
            P(),
            P(None, None, "tensor"),
            P(None, "tensor"),
            P(None, "tensor"),
            P("tensor", None),
            P(),
            P(),
            P(),
            P(None, "tensor"),
            P("tensor"),
            P("tensor", None),
            P(),
            P(),
            P(),
            P("dp", None),
        ),
        out_specs=(
            P("dp", None),
            P("dp", None),
            P(),
            P(),
            P(None, None, "tensor"),
            P(None, "tensor"),
            P(None, "tensor"),
            P("tensor", None),
            P(),
            P(),
            P(),
            P(None, "tensor"),
            P("tensor"),
            P("tensor", None),
            P(),
        ),
        check_vma=False,
    )
```

profile of v0, /device:TPU:0, one launch (start us, length us, event | category | flops | bytes accessed | tf_op | source)
XLA Modules:
  0.0 377.0 jit_solution(15921145427322588425)
XLA Ops:
  7.2 1.1 convert_reduce_fusion
  8.4 1.1 fusion.33
  9.5 1.1 fusion.27
  11.5 0.9 eq.32
  12.4 1.5 compare_select_fusion
  13.9 1.9 convolution_bitcast_fusion
  16.0 0.8 copy.81
  18.6 1.0 copy.82
  20.2 1.5 exponential_reduce_fusion
  21.7 1.3 fusion.6
  23.8 0.9 copy.84
  24.7 1.2 reshape.237
  26.5 0.8 reshape.238
  27.3 2.2 copy.85
  29.6 21.2 %all-reduce.8.cloned.1.call-done = f32[1,14,14,512]{3,0,2,1:T(1,128)} async-done(((f32[1,14,14,512]{3,0,2,1:T(1,128)}), f32[1,14,14,512]{3,0,2,1:T(1,128)}) %all-reduce.8.cloned.1.call-update) | async-done | bytes 401424 | tf_op jit(solution)/shard_map/psum | solution.py:128
  50.8 0.9 slice.103
  51.7 1.2 slice.104
  52.9 1.8 fusion.38
  54.8 1.1 reshape.240
  57.1 1.2 fusion.66
  59.1 1.3 fusion.57
  60.6 2.4 fusion.68
  63.0 1.9 fusion.55
  64.9 15.3 %all-reduce.10.cloned.1.call-done = f32[196,512]{1,0:T(8,128)} async-done(((f32[196,512]{1,0:T(8,128)}), f32[196,512]{1,0:T(8,128)}) %all-reduce.10.cloned.1.call-update) | async-done | bytes 401424 | tf_op jit(solution)/shard_map/psum | solution.py:143
  80.2 1.9 multiply_reduce_fusion.1
  82.0 2.6 fusion.59
  84.7 1.7 reshape.241
  86.4 0.8 slice.106
  87.2 0.9 slice.105
  89.0 1.7 convert_element_type.125
  90.6 1.6 copy.86
  92.3 1.7 convert_element_type.127
  94.0 1.9 convolution_convert_fusion.2
  95.9 1.9 reshape.252
  97.8 2.0 reshape.248
  99.9 2.0 copy.88
  101.8 2.3 copy.91
  104.1 1.3 multiply_reduce_fusion
  105.4 1.4 fusion.63
  106.8 1.2 fusion.65
  108.0 1.1 fusion.7
  109.0 1.0 fusion.62
  110.0 0.9 copy.101
  110.9 1.2 convert_element_type.141
  112.1 1.9 copy.98
  113.9 1.2 convert_element_type.138
  115.1 1.9 copy.95
  117.0 1.2 convert_element_type.134
  118.7 1.2 convolution_add_fusion.2
  120.6 1.1 fusion.36
  122.6 1.8 fusion.70
  125.2 1.3 pad_maximum_fusion
  126.5 1.0 fusion.69
  128.8 0.9 fusion
  129.7 13.3 %all-reduce.14.cloned.1.call-done = (f32[196,512]{1,0:T(8,128)}, f32[196,512]{1,0:T(8,128)}) async-done(((f32[196,512]{1,0:T(8,128)}, f32[196,512]{1,0:T(8,128)}), (f32[196,512]{1,0:T(8,128)}, f32[196,512]{1,0:T(8,128)})) %all-reduce.14.cloned.1.call-update) | async-done | bytes 802832 | tf_op jit(solution)/shard_map/psum | solution.py:134
  143.0 1.4 fusion.32
  144.5 80.1 %all-reduce = (f32[512]{0:T(512)}, f32[512]{0:T(512)}, f32[2,256]{1,0:T(2,128)}, f32[169,8]{0,1:T(8,128)}, f32[512]{0:T(512)}, /*index=5*/f32[512]{0:T(512)}, f32[512]{0:T(512)}, f32[1024]{0:T(1024)}, f32[512]{0:T(512)}) all-reduce(f32[512]{0:T(512)S(1)} %get-tuple-element.17, ...), channel_id=1, replica_groups=mesh['dp'=16,'tensor'=2] {'dp'}, use_global_device_ids=true, to_apply=%region_15.16 | all-reduce | flops 5960 | bytes 47680 | tf_op jit(solution)/shard_map/psum | solution.py:192
  224.5 1.8 add_add_fusion
  226.4 0.9 fusion.31
  227.3 135.8 %all-reduce.12.cloned.1.call-done = (f32[3,512,256]{2,1,0:T(8,128)}, f32[256,512]{1,0:T(8,128)}, f32[512,1024]{1,0:T(8,128)}, f32[1024,512]{1,0:T(8,128)}) async-done(((f32[3,512,256]{2,1,0:T(8,128)}, f32[256,512]{1,0:T(8,128)}, f32[512,1024]{1,0:T(8,128)}, f32[1024,512]{1,0:T(8,128)}), (f32[3,512,256]{2,1,0:T(8,128)}, f32[256,512]{1,0:T(8,128)}, f32[512,1024]{1,0:T(8,128)}, ...) | async-done | bytes 6291472 | tf_op jit(solution)/shard_map/psum | solution.py:192
  363.1 2.8 copy.129
  366.8 1.3 copy.131
  368.1 1.0 copy-done.6
  369.1 1.3 copy.132
  (131 shorter events, 12.7 us)
Async XLA Ops:
  7.2 49.1 %copy-start = (bf16[512,1024]{1,0:T(8,128)(2,1)S(1)}, bf16[512,1024]{1,0:T(8,128)(2,1)}, u32[]{:S(2)}) copy-start(bf16[512,1024]{1,0:T(8,128)(2,1)} %param.27) | copy-start | bytes 3145732
  7.2 43.6 %all-reduce.8.cloned.1.call-start = ((), (), s32[]{:S(2)}) async-start(), calls=%async_computation | async-start | bytes 802816 | tf_op jit(solution)/shard_map/psum | solution.py:128
  10.8 6.4 %copy-start.12 = (bf16[3,512,256]{2,1,0:T(8,128)(2,1)S(1)}, bf16[3,512,256]{2,1,0:T(8,128)(2,1)}, u32[]{:S(2)}) copy-start(bf16[3,512,256]{2,1,0:T(8,128)(2,1)} %param.20) | copy-start | bytes 2359300
  12.4 1.5 copy-start.27
  17.6 2.6 copy-start.24
  20.2 2.8 copy-start.3
  21.7 4.1 %copy-start.17 = (bf16[256,512]{1,0:T(8,128)(2,1)S(1)}, bf16[256,512]{1,0:T(8,128)(2,1)}, u32[]{:S(2)}) copy-start(bf16[256,512]{1,0:T(8,128)(2,1)} %param.23) | copy-start | bytes 786436
  23.0 0.7 copy-start.18
  25.8 0.6 copy-start.14
  27.3 28.5 %copy-start.1 = (bf16[196,512]{1,0:T(8,128)(2,1)S(1)}, bf16[196,512]{1,0:T(8,128)(2,1)}, u32[]{:S(2)}) copy-start(bf16[196,512]{1,0:T(8,128)(2,1)} %param.17) | copy-start | bytes 602116
  27.3 28.5 %copy-start.36 = (f32[512]{0:T(512)S(1)}, f32[512]{0:T(512)}, u32[]{:S(2)}) copy-start(f32[512]{0:T(512)} %param.24) | copy-start | bytes 6148
  29.5 26.7 %copy-start.25 = (f32[512]{0:T(512)S(1)}, f32[512]{0:T(512)}, u32[]{:S(2)}) copy-start(f32[512]{0:T(512)} %param.25) | copy-start | bytes 6148
  29.6 26.7 %copy-start.29 = (f32[512]{0:T(512)S(1)}, f32[512]{0:T(512)}, u32[]{:S(2)}) copy-start(f32[512]{0:T(512)} %param.26) | copy-start | bytes 6148
  29.6 26.7 %copy-start.34 = (f32[1024]{0:T(1024)S(1)}, f32[1024]{0:T(1024)}, u32[]{:S(2)}) copy-start(f32[1024]{0:T(1024)} %param.28) | copy-start | bytes 12292
  29.6 50.6 %all-reduce.10.cloned.1.call-start = ((), (), s32[]{:S(2)}) async-start(), calls=%async_computation.1 | async-start | bytes 819200 | tf_op jit(solution)/shard_map/psum | solution.py:143
  55.9 1.2 copy-start.16
  55.9 1.2 copy-start.21
  58.3 0.8 copy-start.9
  60.3 82.7 %all-reduce.14.cloned.1.call-start = ((), (), s32[]{:S(2)}) async-start(), calls=%async_computation.3 | async-start | bytes 1638400 | tf_op jit(solution)/shard_map/psum | solution.py:134
  60.6 2.4 copy-start.10
  104.1 2.7 copy-start.5
  104.1 2.7 copy-start.19
  104.1 3.9 %copy-start.4 = (bf16[4,49,8,32]{1,3,2,0:T(8,128)(2,1)S(1)}, bf16[4,49,8,32]{1,3,2,0:T(8,128)(2,1)}, u32[]{:S(2)}) copy-start(bf16[4,49,8,32]{1,3,2,0:T(8,128)(2,1)} %copy-done.3) | copy-start | bytes 301060
  109.0 9.1 %copy-start.13 = (bf16[3,512,256]{2,1,0:T(8,128)(2,1)S(1)}, bf16[3,512,256]{2,1,0:T(8,128)(2,1)}, u32[]{:S(2)}) copy-start(bf16[3,512,256]{2,1,0:T(8,128)(2,1)} %param.20) | copy-start | bytes 2359300
  119.9 2.6 copy-start.22
  122.5 240.6 %all-reduce.12.cloned.1.call-start = ((), (), s32[]{:S(2)}) async-start(), calls=%async_computation.2 | async-start | bytes 12582912 | tf_op jit(solution)/shard_map/psum | solution.py:192
  124.9 1.5 copy-start.8
  124.9 1.5 copy-start.15
  127.5 0.9 copy-start.20
  127.5 1.3 copy-start.28
  127.5 15.5 %copy-start.26 = (f32[512]{0:T(512)S(1)}, f32[512]{0:T(512)}, u32[]{:S(2)}) copy-start(f32[512]{0:T(512)} %param.18) | copy-start | bytes 6148
  127.5 16.9 %copy-start.30 = (f32[512]{0:T(512)S(1)}, f32[512]{0:T(512)}, u32[]{:S(2)}) copy-start(f32[512]{0:T(512)} %get-tuple-element.15) | copy-start | bytes 6148
  127.5 16.9 %copy-start.31 = (f32[512]{0:T(512)S(1)}, f32[512]{0:T(512)}, u32[]{:S(2)}) copy-start(f32[512]{0:T(512)} %get-tuple-element.21) | copy-start | bytes 6148
  127.5 16.9 %copy-start.32 = (f32[512]{0:T(512)S(1)}, f32[512]{0:T(512)}, u32[]{:S(2)}) copy-start(f32[512]{0:T(512)} %get-tuple-element.38) | copy-start | bytes 6148
  127.5 16.9 %copy-start.33 = (f32[512]{0:T(512)S(1)}, f32[512]{0:T(512)}, u32[]{:S(2)}) copy-start(f32[512]{0:T(512)} %get-tuple-element.46) | copy-start | bytes 6148
  127.6 16.9 %copy-start.35 = (f32[1024]{0:T(1024)S(1)}, f32[1024]{0:T(1024)}, u32[]{:S(2)}) copy-start(f32[1024]{0:T(1024)} %get-tuple-element.57) | copy-start | bytes 12292
  127.6 96.9 %copy-start.37 = (f32[512]{0:T(512)S(1)}, f32[512]{0:T(512)}, u32[]{:S(2)}) copy-start(f32[512]{0:T(512)} %param.30) | copy-start | bytes 6148
  127.6 98.7 %copy-start.2 = (f32[196,512]{1,0:T(8,128)S(1)}, f32[196,512]{1,0:T(8,128)}, u32[]{:S(2)}) copy-start(f32[196,512]{1,0:T(8,128)} %get-tuple-element.39) | copy-start | bytes 1204228
  143.0 83.3 %copy-start.11 = (f32[196,512]{1,0:T(8,128)S(1)}, f32[196,512]{1,0:T(8,128)}, u32[]{:S(2)}) copy-start(f32[196,512]{1,0:T(8,128)} %get-tuple-element.37) | copy-start | bytes 1204228
  363.1 2.8 copy-start.23
  363.1 3.6 copy-start.7
  366.8 2.3 copy-start.6
Sparse Core Ops, SparseCore 0:
  29.7 21.1 all-reduce.7
  60.5 19.6 all-reduce.9
  122.6 20.3 all-reduce.13
  150.5 212.6 all-reduce.11
where the time goes:
time: 378 us; the launch traced here: 377 us
  waiting for transfers between devices  186 us (49%)
  blocking collectives  80.1 us (21%)
  local copies, waits for them, and re-layouts  50.5 us (13%)
  matrix products  25.6 us (7%)
  other arithmetic  20.3 us (5%)
  between operations  14.5 us (4%)
    psum x1, waiting for transfers between devices, body(): lax.psum((g_ln1_gain, g_ln1_bias, g_qkv, g_qv_bias, g_table, g_proj, g_pr...  136 us
    psum x1, blocking collectives, body(): lax.psum((g_ln1_gain, g_ln1_bias, g_qkv, g_qv_bias, g_table, g_proj, g_pr...  80.1 us
    psum x1, waiting for transfers between devices, body(): lax.psum(jnp.dot(attn_flat, w_proj, preferred_element_type=jnp.float32),...  21.2 us
    psum x1, waiting for transfers between devices, body(): dcn = lax.psum(outer(dub, w_fc1), 'tensor')  15.3 us
    psum x1, waiting for transfers between devices, body(): lax.psum(jnp.dot(zact, w_fc2, preferred_element_type=jnp.float32), 'tensor')  13.3 us
    unnamed x80, local copies, waits for them, and re-layouts  10.4 us
  transfers between devices with their start and end apart: 4, of which 4 were waited for; matrix products, arithmetic and copies ran while one was open for 4% of the time, Pallas kernels for 0%

commit v1 on v0

v1 whole, which is shorter than its diff:
```python
import functools

import jax
import jax.numpy as jnp
import numpy as np
from jax import lax
from jax.experimental import pallas as pl
from jax.experimental.pallas import tpu as pltpu
from jax.sharding import PartitionSpec as P

SIDE = 14
WIN = 7
SHIFT = 3
NWIN = 4
WTOK = 49
WPAD = 64
TABLE = 169
BLOCKS = 16
F32 = jnp.float32
BF16 = jnp.bfloat16

ORDERS = ((2, 4, 1, 8), (4, 1, 8, 2), (1, 2, 4, 8))


def dot(left, right, dims=((1,), (0,))):
    return lax.dot_general(left, right, (dims, ((), ())), preferred_element_type=F32)


NT = ((1,), (1,))
TN = ((0,), (0,))


def window_rows(nimg):
    per = SIDE // WIN
    rows = np.zeros((nimg * NWIN * WPAD, nimg * SIDE * SIDE), np.float32)
    for img in range(nimg):
        for win in range(NWIN):
            for pos in range(WTOK):
                r = (win // per) * WIN + pos // WIN
                c = (win % per) * WIN + pos % WIN
                src = ((r + SHIFT) % SIDE) * SIDE + (c + SHIFT) % SIDE
                rows[(img * NWIN + win) * WPAD + pos, img * SIDE * SIDE + src] = 1.0
    return rows


def stats(values):
    mean = jnp.mean(values, -1, keepdims=True)
    centred = values - mean
    var = jnp.mean(centred * centred, -1, keepdims=True)
    rstd = lax.rsqrt(var + 1e-05)
    return centred * rstd, rstd


def norm_back(dout, nhat, rstd, gain):
    dnorm = dout * gain
    return rstd * (
        dnorm
        - jnp.mean(dnorm, -1, keepdims=True)
        - nhat * jnp.mean(dnorm * nhat, -1, keepdims=True)
    )


def head_mask(heads, width):
    hdim = width // heads
    row = lax.broadcasted_iota(jnp.int32, (heads * WPAD, width), 0) // WPAD
    col = lax.broadcasted_iota(jnp.int32, (heads * WPAD, width), 1) // hdim
    return jnp.where(row == col, 1.0, 0.0).astype(F32)


def position_bias(table_ref, rel_ref, tab_s, idx_s, bias_s, heads):
    tab_s[...] = jnp.zeros_like(tab_s)
    tab_s[0:TABLE, 0:heads] = table_ref[...]
    idx_s[...] = jnp.zeros_like(idx_s)
    idx_s[0:WTOK, 0:WTOK] = rel_ref[...]
    flipped = tab_s[...].T
    idx = idx_s[...]
    low = idx & 127
    first = idx < 128
    pad = lax.broadcasted_iota(jnp.int32, (WPAD, WPAD), 1) >= WTOK
    for h in range(heads):
        a = jnp.take_along_axis(jnp.broadcast_to(flipped[h : h + 1, 0:128], (WPAD, 128)), low, axis=1)
        b = jnp.take_along_axis(jnp.broadcast_to(flipped[h : h + 1, 128:256], (WPAD, 128)), low, axis=1)
        got = jnp.where(first, a, b)[:, 0:WPAD]
        bias_s[h * WPAD : (h + 1) * WPAD, :] = jnp.where(pad, -1e30, got)


def region_mask(rid_ref, rid_s):
    rid_s[...] = jnp.zeros_like(rid_s)
    rid_s[0:NWIN, 0:WTOK] = rid_ref[...].astype(F32)
    rows = rid_s[...]
    cols = rows.T
    out = []
    for w in range(NWIN):
        same = cols[0:WPAD, w : w + 1] == rows[w : w + 1, 0:WPAD]
        out.append(jnp.where(same, 0.0, -100.0).astype(F32))
    return out


def by_head(values, mask, heads):
    return jnp.concatenate([values] * heads, 0) * mask


def over_heads(values, mask, heads):
    kept = values * mask
    total = kept[0:WPAD]
    for h in range(1, heads):
        total = total + kept[h * WPAD : (h + 1) * WPAD]
    return total


def probabilities(qb, kw, bias, mask, heads):
    s = dot(qb, kw, NT) + bias + jnp.concatenate([mask] * heads, 0)
    e = jnp.exp(s)
    return e / jnp.sum(e, -1, keepdims=True)


def attend_kernel(
    x_ref, gain_ref, shift_ref, wqkv_ref, qvb_ref, table_ref, rel_ref, rid_ref, wproj_ref, pw_ref, pwt_ref,
    part_ref, q_ref, k_ref, v_ref, o_ref,
    tab_s, idx_s, bias_s, rid_s, ow_s, hm_s,
):
    heads = table_ref.shape[1]
    width = wqkv_ref.shape[2]
    scale = (width // heads) ** (-0.5)
    nhat, _ = stats(x_ref[...].astype(F32))
    a = (nhat * gain_ref[...] + shift_ref[...]).astype(BF16)
    pw = pw_ref[...]
    q = ((dot(a, wqkv_ref[0]) + qvb_ref[0:1, :]) * scale).astype(BF16)
    q_ref[...] = dot(pw, q).astype(BF16)
    k = dot(a, wqkv_ref[1]).astype(BF16)
    k_ref[...] = dot(pw, k).astype(BF16)
    v = (dot(a, wqkv_ref[2]) + qvb_ref[1:2, :]).astype(BF16)
    v_ref[...] = dot(pw, v).astype(BF16)
    position_bias(table_ref, rel_ref, tab_s, idx_s, bias_s, heads)
    masks = region_mask(rid_ref, rid_s)
    hm_s[...] = head_mask(heads, width)
    bias = bias_s[...]
    hm = hm_s[...]
    hmb = hm.astype(BF16)
    for w in range(q_ref.shape[0] // WPAD):
        rows = slice(w * WPAD, (w + 1) * WPAD)
        qb = by_head(q_ref[rows, :], hmb, heads)
        p = probabilities(qb, k_ref[rows, :], bias, masks[w % NWIN], heads)
        full = dot(p.astype(BF16), v_ref[rows, :])
        ow_s[rows, :] = over_heads(full, hm, heads).astype(BF16)
    o = dot(pwt_ref[...], ow_s[...]).astype(BF16)
    o_ref[...] = o
    part_ref[...] = dot(o, wproj_ref[...])


def mlp_kernel(
    me_ref, x_ref, own_ref, other_ref, pbias_ref, gain_ref, shift_ref, w1_ref, b1_ref, w2_ref, cot_ref,
    h_ref, mlp_ref, dc_ref, small_ref, s0lo, s0hi, s1lo, s1hi, s2lo, s2hi,
    g1_s, g2_s,
):
    hid = w1_ref.shape[1]
    dim = w1_ref.shape[0]
    h = x_ref[...].astype(F32) + own_ref[...] + other_ref[...] + pbias_ref[...]
    h_ref[...] = h
    nhat, _ = stats(h)
    c = (nhat * gain_ref[...] + shift_ref[...]).astype(BF16)
    cot = cot_ref[...]
    small_ref[0:1, :] = jnp.sum(cot.astype(F32), 0, keepdims=True)
    step = 256
    mlp = jnp.zeros(h.shape, F32)
    dc = jnp.zeros(h.shape, F32)
    for j in range(hid // step):
        cols = slice(j * step, (j + 1) * step)
        w1 = w1_ref[:, cols]
        w2 = w2_ref[cols, :]
        u = dot(c, w1) + b1_ref[:, cols]
        cdf = 0.5 * (1.0 + lax.erf(u * 0.7071067811865476))
        z = (u * cdf).astype(BF16)
        slope = cdf + u * jnp.exp(-0.5 * u * u) * 0.3989422804014327
        du = dot(cot, w2, NT) * slope
        at = (j * step) % dim
        small_ref[1 + (j * step) // dim : 2 + (j * step) // dim, at : at + step] = jnp.sum(du, 0, keepdims=True)
        dub = du.astype(BF16)
        g2_s[cols, :] = dot(z, cot, TN)
        g1_s[:, cols] = dot(c, dub, TN)
        mlp = mlp + dot(z, w2)
        dc = dc + dot(dub, w1, NT)
    mlp_ref[...] = mlp
    dc_ref[...] = dc
    fill_streams(me_ref[0], STREAMS_A, ((s0lo, s0hi), (s1lo, s1hi), (s2lo, s2hi)), (g1_s, g2_s))


def tail_kernel(
    me_ref, own_ref, other_ref, mown_ref, mother_ref, fbias_ref, h_ref, x_ref, cot_ref, gain2_ref, gain1_ref, shift1_ref,
    wqkv_ref, wproj_ref, q_ref, k_ref, v_ref, o_ref, table_ref, rel_ref, rid_ref, pw_ref, pwt_ref,
    out_ref, dh_ref, da_ref, small_ref, dbias_ref, s0lo, s0hi, s1lo, s1hi, s2lo, s2hi,
    tab_s, idx_s, bias_s, rid_s, hm_s, dq_s, dk_s, dv_s, gq_s, gp_s,
):
    heads = table_ref.shape[1]
    width = wqkv_ref.shape[2]
    scale = (width // heads) ** (-0.5)
    h = h_ref[...]
    out_ref[...] = h + mown_ref[...] + mother_ref[...] + fbias_ref[...]
    dc = own_ref[...] + other_ref[...]
    nhat2, rstd2 = stats(h)
    dh = cot_ref[...].astype(F32) + norm_back(dc, nhat2, rstd2, gain2_ref[...])
    dh_ref[...] = dh
    small_ref[0:1, :] = jnp.sum(dh, 0, keepdims=True)
    small_ref[1:2, :] = jnp.sum(dc * nhat2, 0, keepdims=True)
    small_ref[2:3, :] = jnp.sum(dc, 0, keepdims=True)
    dhb = dh.astype(BF16)
    gp_s[...] = dot(o_ref[...], dhb, TN)
    do = dot(dhb, wproj_ref[...], NT).astype(BF16)
    dow = dot(pw_ref[...], do).astype(BF16)
    position_bias(table_ref, rel_ref, tab_s, idx_s, bias_s, heads)
    masks = region_mask(rid_ref, rid_s)
    hm_s[...] = head_mask(heads, width)
    bias = bias_s[...]
    hm = hm_s[...]
    hmb = hm.astype(BF16)
    dbias = jnp.zeros(bias.shape, F32)
    sum_q = jnp.zeros((1, width), F32)
    sum_v = jnp.zeros((1, width), F32)
    for w in range(q_ref.shape[0] // WPAD):
        rows = slice(w * WPAD, (w + 1) * WPAD)
        kw = k_ref[rows, :]
        qb = by_head(q_ref[rows, :], hmb, heads)
        p = probabilities(qb, kw, bias, masks[w % NWIN], heads)
        db = by_head(dow[rows, :], hmb, heads)
        dp = dot(db, v_ref[rows, :], NT)
        ds = p * (dp - jnp.sum(p * dp, -1, keepdims=True))
        dbias = dbias + ds
        dv = dot(p.astype(BF16), db, TN)
        dsb = ds.astype(BF16)
        dq = over_heads(dot(dsb, kw), hm, heads) * scale
        dk = dot(dsb, qb, TN)
        sum_q = sum_q + jnp.sum(dq, 0, keepdims=True)
        sum_v = sum_v + jnp.sum(dv, 0, keepdims=True)
        dq_s[rows, :] = dq.astype(BF16)
        dk_s[rows, :] = dk.astype(BF16)
        dv_s[rows, :] = dv.astype(BF16)
    dbias_ref[...] = dbias
    small_ref[3:4, 0:width] = sum_q
    small_ref[3:4, width : 2 * width] = sum_v
    nhat1, _ = stats(x_ref[...].astype(F32))
    a = (nhat1 * gain1_ref[...] + shift1_ref[...]).astype(BF16)
    pwt = pwt_ref[...]
    da = jnp.zeros(h.shape, F32)
    for m, ref in enumerate((dq_s, dk_s, dv_s)):
        d = dot(pwt, ref[...]).astype(BF16)
        gq_s[m] = dot(a, d, TN)
        da = da + dot(d, wqkv_ref[m], NT)
    da_ref[...] = da
    fill_streams(
        me_ref[0], STREAMS_B, ((s0lo, s0hi), (s1lo, s1hi), (s2lo, s2hi)), (gq_s.at[0], gq_s.at[1], gq_s.at[2], gp_s)
    )


def first_kernel(own_ref, other_ref, x_ref, dh_ref, gain_ref, dx_ref, small_ref):
    da = own_ref[...] + other_ref[...]
    nhat, rstd = stats(x_ref[...].astype(F32))
    small_ref[0:1, :] = jnp.sum(da * nhat, 0, keepdims=True)
    small_ref[1:2, :] = jnp.sum(da, 0, keepdims=True)
    dx_ref[...] = dh_ref[...] + norm_back(da, nhat, rstd, gain_ref[...])


STREAMS_A = (
    tuple((0, 32, t) for t in range(0, 5)),
    tuple((0, 32, t) for t in range(5, 8)) + ((1, 64, 0),),
    tuple((1, 64, t) for t in range(1, 4)),
)
STREAMS_B = (
    ((0, 32, 0), (0, 32, 1), (3, 16, 0), (3, 16, 1)),
    ((2, 32, 0), (2, 32, 1)),
    ((1, 32, 0), (1, 32, 1), (3, 16, 2), (3, 16, 3)),
)


def block_at(me, order, place):
    flips = sum(bit for i, bit in enumerate(order) if place & (8 >> i))
    return lax.bitwise_xor(me, jnp.int32(flips))


def stream_rows(stream):
    return sum(rows for _, rows, _ in stream)


def fill_streams(me, streams, halves, grads):
    for stream, (lo, hi), order in zip(streams, halves, ORDERS):
        for place in range(BLOCKS):
            block = block_at(me, order, place)
            half = lo if place < BLOCKS // 2 else hi
            at = 0
            for g, rows, tile in stream:
                src = pl.ds(pl.multiple_of(block * rows, rows), rows)
                half[place % (BLOCKS // 2), at : at + rows, :] = grads[g][src, tile * 128 : (tile + 1) * 128]
                at += rows


def collect_kernel(streams, npieces, me_ref, *refs):
    pieces = refs[: len(streams) * npieces]
    outs = refs[len(streams) * npieces :]
    me = me_ref[0]
    for s, (stream, order) in enumerate(zip(streams, ORDERS)):
        mine = pieces[s * npieces : (s + 1) * npieces]
        places = [(ref, i) for ref in mine for i in range(ref.shape[0])]
        for place, (ref, i) in enumerate(places):
            block = block_at(me, order, place)
            at = 0
            for g, rows, tile in stream:
                dst = pl.ds(pl.multiple_of(block * rows, rows), rows)
                outs[g][dst, tile * 128 : (tile + 1) * 128] = ref[i, at : at + rows, :]
                at += rows


def vmem(n):
    return [pl.BlockSpec(memory_space=pltpu.VMEM) for _ in range(n)]


def smem():
    return pl.BlockSpec(memory_space=pltpu.SMEM)


def call(kernel, outs, args, scratch=(), scalars=0, name=None):
    return pl.pallas_call(
        kernel,
        out_shape=tuple(jax.ShapeDtypeStruct(s, d) for s, d in outs),
        in_specs=[smem() for _ in range(scalars)] + vmem(len(args) - scalars),
        out_specs=tuple(vmem(len(outs))),
        scratch_shapes=[pltpu.VMEM(s, d) for s, d in scratch],
        name=name,
    )(*args)


def swap(values, bit, size):
    return lax.ppermute(values, "dp", [(i, i ^ bit) for i in range(size)])


def partner(values):
    return lax.ppermute(values, "tensor", [(0, 1), (1, 0)])


def reduce_streams(halves, size):
    keep = [lo for lo, _ in halves]
    send = [hi for _, hi in halves]
    for r in range(4):
        got = [swap(s, o[r], size) for s, o in zip(send, ORDERS)]
        h = 8 >> (r + 1)
        if r < 3:
            send = [k[h:] + g[h:] for k, g in zip(keep, got)]
            keep = [k[:h] + g[:h] for k, g in zip(keep, got)]
        else:
            keep = [k + g for k, g in zip(keep, got)]
    bit = BLOCKS
    while bit < size:
        keep = [k + swap(k, bit, size) for k in keep]
        bit *= 2
    pieces = [[k] for k in keep]
    for r in range(3, -1, -1):
        got = [swap(k, o[r], size) for k, o in zip(keep, ORDERS)]
        for p, g in zip(pieces, got):
            p.append(g)
        if r:
            keep = [jnp.concatenate([k, g], 0) for k, g in zip(keep, got)]
    return pieces


def collect(streams, pieces, me, outs, name):
    flat = [p for piece in pieces for p in piece]
    kernel = functools.partial(collect_kernel, streams, len(pieces[0]))
    return call(kernel, outs, [me] + flat, scalars=1, name=name)


def body(
    size,
    block_input,
    ln1_gain,
    ln1_bias,
    w_qkv,
    qv_bias,
    bias_table,
    w_proj,
    proj_bias,
    ln2_gain,
    ln2_bias,
    w_fc1,
    fc1_bias,
    w_fc2,
    fc2_bias,
    region_ids,
    rel_index,
    cotangent,
):
    tokens, dim = block_input.shape
    nimg = tokens // (SIDE * SIDE)
    heads = bias_table.shape[1]
    width = w_qkv.shape[2]
    hid = w_fc1.shape[1]
    wrows = nimg * NWIN * WPAD
    rows_np = window_rows(nimg)
    pw = jnp.asarray(rows_np, BF16)
    pwt = jnp.asarray(rows_np.T, BF16)
    me = lax.bitwise_and(lax.axis_index("dp"), BLOCKS - 1).astype(jnp.int32).reshape(1)
    row = lambda v: v.reshape(1, -1)
    g1, b1, g2, b2 = row(ln1_gain), row(ln1_bias), row(ln2_gain), row(ln2_bias)
    att_scratch = [((256, 128), F32), ((WPAD, 128), jnp.int32), ((heads * WPAD, WPAD), F32), ((128, 128), F32)]
    tok = ((tokens, dim), F32)
    win = ((wrows, width), BF16)

    part, qw, kw, vw, otok = call(
        attend_kernel,
        [tok, win, win, win, ((tokens, width), BF16)],
        [block_input, g1, b1, w_qkv, qv_bias, bias_table, rel_index, region_ids, w_proj, pw, pwt],
        att_scratch + [win, ((heads * WPAD, width), F32)],
        name="attend",
    )
    other = partner(part)

    def halves(streams):
        return [((BLOCKS // 2, stream_rows(s), 128), F32) for s in streams for _ in range(2)]

    h, mlp, dc, small2, *sa = call(
        mlp_kernel,
        [tok, tok, tok, ((1 + hid // dim, dim), F32)] + halves(STREAMS_A),
        [me, block_input, part, other, row(proj_bias), g2, b2, w_fc1, row(fc1_bias), w_fc2, cotangent],
        [((dim, hid), F32), ((hid, dim), F32)],
        scalars=1,
        name="mlp",
    )
    dc_other = partner(dc)
    mlp_other = partner(mlp)
    pieces_a = reduce_streams(list(zip(sa[0::2], sa[1::2])), size)

    out, dh, da, small3, dbias, *sb = call(
        tail_kernel,
        [tok, tok, tok, ((4, dim), F32), ((heads * WPAD, WPAD), F32)] + halves(STREAMS_B),
        [me, dc, dc_other, mlp, mlp_other, row(fc2_bias), h, block_input, cotangent, g2, g1, b1]
        + [w_qkv, w_proj, qw, kw, vw, otok, bias_table, rel_index, region_ids, pw, pwt],
        att_scratch + [((heads * WPAD, width), F32), win, win, win, ((3, dim, width), F32), ((width, dim), F32)],
        scalars=1,
        name="tail",
    )
    da_other = partner(da)
    pieces_b = reduce_streams(list(zip(sb[0::2], sb[1::2])), size)
    dx, small4 = call(first_kernel, [tok, ((2, dim), F32)], [da, da_other, block_input, dh, g1], name="first")

    onehot = (rel_index.reshape(-1)[:, None] == lax.iota(jnp.int32, TABLE)[None, :]).astype(F32)
    flat = dbias.reshape(heads, WPAD, WPAD)[:, :WTOK, :WTOK].reshape(heads, WTOK * WTOK)
    g_table = lax.dot_general(onehot, flat, (((0,), (1,)), ((), ())), precision=lax.Precision.HIGHEST)
    nt = -(-TABLE * heads // dim)
    table_rows = jnp.pad(g_table.reshape(-1), (0, nt * dim - TABLE * heads)).reshape(nt, dim)
    small = jnp.concatenate([small2, small3, small4, table_rows], 0)
    bit = 1
    while bit < size:
        small = small + swap(small, bit, size)
        bit *= 2

    g_fc1, g_fc2 = collect(STREAMS_A, pieces_a, me, [((dim, hid), F32), ((hid, dim), F32)], "collect_mlp")
    gq, gk, gv, g_proj = collect(
        STREAMS_B, pieces_b, me, [((dim, width), F32)] * 3 + [((width, dim), F32)], "collect_att"
    )
    g_qkv = jnp.stack([gq, gk, gv])
    n2 = 1 + hid // dim
    return (
        out,
        dx,
        small[n2 + 4],
        small[n2 + 5],
        g_qkv,
        small[n2 + 3].reshape(2, width),
        small[n2 + 6 :].reshape(-1)[: TABLE * heads].reshape(TABLE, heads),
        g_proj,
        small[n2],
        small[n2 + 1],
        small[n2 + 2],
        g_fc1,
        small[1:n2].reshape(-1),
        g_fc2,
        small[0],
    )


def solution(mesh):
    return jax.shard_map(
        functools.partial(body, mesh.shape["dp"]),
        mesh=mesh,
        in_specs=(
            P("dp", None),
            P(),
            P(),
            P(None, None, "tensor"),
            P(None, "tensor"),
            P(None, "tensor"),
            P("tensor", None),
            P(),
            P(),
            P(),
            P(None, "tensor"),
            P("tensor"),
            P("tensor", None),
            P(),
            P(),
            P(),
            P("dp", None),
        ),
        out_specs=(
            P("dp", None),
            P("dp", None),
            P(),
            P(),
            P(None, None, "tensor"),
            P(None, "tensor"),
            P(None, "tensor"),
            P("tensor", None),
            P(),
            P(),
            P(),
            P(None, "tensor"),
            P("tensor"),
            P("tensor", None),
            P(),
        ),
        check_vma=False,
    )
```

time: 378 us -> 196 us (0.52)
  waiting for transfers between devices: 186 us -> 78.5 us
  blocking collectives: 80.1 us -> 0 us
  starting transfers between devices: 0.34 us -> 57.7 us
  local copies, waits for them, and re-layouts: 50.5 us -> 10.2 us
  Pallas kernels: 0 us -> 29.2 us
  matrix products: 25.6 us -> 1.9 us
  between operations: 14.5 us -> 1.25 us
  other arithmetic: 20.3 us -> 16.3 us
    psum x4 -> x0, waiting for transfers between devices: 186 us -> none  [the longest x1 136 us: body(): lax.psum((g_ln1_gain, g_ln1_bias, g_qkv, g_qv_bias, g_table, g_proj, g_pr...]
    psum x1 -> x0, blocking collectives: 80.1 us -> none  [body(): lax.psum((g_ln1_gain, g_ln1_bias, g_qkv, g_qv_bias, g_table, g_proj, g_pr...]
    ppermute x0 -> x56, waiting for transfers between devices: none -> 78.5 us  [the longest x52 76.9 us: swap(): return lax.ppermute(values, 'dp', [(i, i ^ bit) for i in range(size)])]
    ppermute x0 -> x56, starting transfers between devices: none -> 57.7 us  [the longest x52 56.7 us: swap(): return lax.ppermute(values, 'dp', [(i, i ^ bit) for i in range(size)])]
    pallas_call x0 -> x6, Pallas kernels: none -> 29.2 us  [call(): pl.pallas_call(kernel, out_shape=tuple((jax.ShapeDtypeStruct(s, d) for s,...]
    dot_general x26 -> x1, matrix products: 25.6 us -> 1.9 us  [body(): lax.dot_general(onehot, flat, (((0,), (1,)), ((), ())), precision=lax.Pre...]
    convert_element_type x12 -> x0, local copies, waits for them, and re-layouts: 18.3 us -> none  [the longest x3 5.02 us: body(): dhw = to_windows(dh, nimg).astype(jnp.bfloat16)]
    reduce_sum x8 -> x0, other arithmetic: 9.76 us -> none  [the longest x1 2.62 us: body(): g_proj_bias = jnp.sum(dh, 0)]
  transfers between devices with their start and end apart: 4 -> 56, of which waited for: 4 -> 24; matrix products, arithmetic and copies ran while one was open for 4% -> 11% of each run, Pallas kernels for 0% -> 7%
where the time goes in v1:
time: 196 us; the launch traced here: 195 us
  waiting for transfers between devices  78.5 us (40%)
  starting transfers between devices  57.7 us (29%)
  Pallas kernels  29.2 us (15%)
  other arithmetic  16.3 us (8%)
  local copies, waits for them, and re-layouts  10.2 us (5%)
    ppermute x52, waiting for transfers between devices, swap(): return lax.ppermute(values, 'dp', [(i, i ^ bit) for i in range(size)])  76.9 us
    ppermute x52, starting transfers between devices, swap(): return lax.ppermute(values, 'dp', [(i, i ^ bit) for i in range(size)])  56.7 us
    pallas_call x6, Pallas kernels, call(): pl.pallas_call(kernel, out_shape=tuple((jax.ShapeDtypeStruct(s, d) for s,...  29.2 us
    add x12, other arithmetic, reduce_streams(): keep = [k[:h] + g[:h] for k, g in zip(keep, got)]  8.39 us
    unnamed x88, local copies, waits for them, and re-layouts  7.62 us
  transfers between devices with their start and end apart: 56, of which 24 were waited for; matrix products, arithmetic and copies ran while one was open for 11% of the time, Pallas kernels for 7%

profile of v1, /device:TPU:0, one launch (start us, length us, event | category | flops | bytes accessed | tf_op | source)
XLA Modules:
  0.0 195.0 jit_solution(15863586083516839688)
XLA Ops:
  0.6 1.4 copy.37.table_ref
  2.1 4.3 %attend.1 = (f32[196,512]{1,0:T(8,128)}, bf16[256,256]{1,0:T(8,128)(2,1)}, bf16[256,256]{1,0:T(8,128)(2,1)}, bf16[256,256]{1,0:T(8,128)(2,1)}, bf16[196,256]{1,0:T(8,128)(2,1)}) custom-call(bf16[196,512]{1,0:T(8,128)(2,1)} %x_ref.7, f32[1,512]{1,0:T(1,128)} %bitcast.26, f32[1,512]{1,0:T(1,128)} %bitcast.29, bf16[3,512,256]{2,1,0:T(8,128)(2,1)} %wqkv_ref.3, ...), custom_call_target="tpu_custom_call" | custom-call | tf_op jit(solution)/shard_map/attend/pallas_call | solution.py:320
  6.9 1.6 collective-permute-done.other_ref
  9.3 7.1 %mlp.1 = (f32[196,512]{1,0:T(8,128)}, f32[196,512]{1,0:T(8,128)}, f32[196,512]{1,0:T(8,128)}, f32[3,512]{1,0:T(4,128)}, f32[8,160,128]{2,1,0:T(8,128)}, /*index=...) custom-call(s32[1]{0:T(128)} %bitcast.me_ref, ...), custom_call_target="tpu_custom_call" | custom-call | tf_op jit(solution)/shard_map/mlp/pallas_call | solution.py:320
  16.4 2.9 %collective-permute-start.40 = (f32[8,160,128]{2,1,0:T(8,128)}, f32[8,160,128]{2,1,0:T(8,128)}, u32[]{:S(2)}, u32[]{:S(2)}) collective-permute-start(f32[8,160,128]{2,1,0:T(8,128)} %get-tuple-element.78), channel_id=1, source_target_pairs={{0,8},{2,10},{4,12},{6,14},{8,0},{10,2},{12,4},{14,6},{16,24},{18,... | collective-permute-start | bytes 1966088 | tf_op jit(solution)/shard_map/ppermute | solution.py:331
  20.0 1.6 collective-permute-start.48
  21.5 1.5 collective-permute-start.32
  23.9 7.6 %tail.1 = (f32[196,512]{1,0:T(8,128)}, f32[196,512]{1,0:T(8,128)}, f32[196,512]{1,0:T(8,128)}, f32[4,512]{1,0:T(4,128)}, f32[512,64]{1,0:T(8,128)}, /*index=5*/f...) custom-call(s32[1]{0:T(128)} %bitcast.me_ref, ...), custom_call_target="tpu_custom_call" | custom-call | tf_op jit(solution)/shard_map/tail/pallas_call | solution.py:320
  33.7 1.9 fusion.1
  35.8 1.2 collective-permute-start.8
  37.0 1.9 slice_add_fusion.3
  38.9 1.3 collective-permute-done.16
  40.3 1.7 collective-permute-start.17
  42.0 1.9 slice_add_fusion.5
  44.3 2.4 %first.1 = (f32[196,512]{1,0:T(8,128)}, f32[2,512]{1,0:T(2,128)}) custom-call(f32[196,512]{1,0:T(8,128)} %get-tuple-element.58.own_ref, f32[196,512]{1,0:T(8,128)} %collective-permute-done.3.other_ref, bf16[196,512]{1,0:T(8,128)(2,1)} %x_ref.7, f32[196,512]{1,0:T(8,128)} %get-tuple-element.59.dh_ref, f32[1,512]{1,0:T(1,128)} %bitcast.28), custom_call_target="tpu_custom_call" | custom-call | tf_op jit(solution)/shard_map/first/pallas_call | solution.py:320
  47.5 4.4 %collective-permute-done.17 = f32[4,64,128]{2,1,0:T(8,128)S(1)} collective-permute-done((f32[4,64,128]{2,1,0:T(8,128)S(1)}, f32[4,64,128]{2,1,0:T(8,128)S(1)}, u32[]{:S(2)}, u32[]{:S(2)}) %collective-permute-start.17) | collective-permute-done | bytes 131104 | tf_op jit(solution)/shard_map/ppermute | solution.py:331
  51.9 1.5 collective-permute-start.4
  53.4 5.2 %collective-permute-done.4 = f32[12,512]{1,0:T(8,128)S(1)} collective-permute-done((f32[12,512]{1,0:T(8,128)S(1)}, f32[12,512]{1,0:T(8,128)S(1)}, u32[]{:S(2)}, u32[]{:S(2)}) %collective-permute-start.4) | collective-permute-done | bytes 24608 | tf_op jit(solution)/shard_map/ppermute | solution.py:331
  58.7 2.6 %collective-permute-start.18 = (f32[2,64,128]{2,1,0:T(8,128)S(1)}, f32[2,64,128]{2,1,0:T(8,128)S(1)}, u32[]{:S(2)}, u32[]{:S(2)}) collective-permute-start(f32[2,64,128]{2,1,0:T(8,128)S(1)} %get-tuple-element.121), channel_id=1, source_target_pairs={{0,16},{2,18},{4,20},{6,22},{8,24},{10,26},{12,28},{14,30},{16,0},... | collective-permute-start | bytes 196616 | tf_op jit(solution)/shard_map/ppermute | solution.py:331
  62.0 1.6 collective-permute-start.5
  63.8 2.1 %collective-permute-done.5 = f32[12,512]{1,0:T(8,128)S(1)} collective-permute-done((f32[12,512]{1,0:T(8,128)S(1)}, f32[12,512]{1,0:T(8,128)S(1)}, u32[]{:S(2)}, u32[]{:S(2)}) %collective-permute-start.5) | collective-permute-done | bytes 24608 | tf_op jit(solution)/shard_map/ppermute | solution.py:331
  66.4 1.6 collective-permute-start.6
  68.1 1.6 collective-permute-start.19
  69.6 1.1 slice_add_fusion.9
  70.7 3.8 %collective-permute-done.6 = f32[12,512]{1,0:T(8,128)S(1)} collective-permute-done((f32[12,512]{1,0:T(8,128)S(1)}, f32[12,512]{1,0:T(8,128)S(1)}, u32[]{:S(2)}, u32[]{:S(2)}) %collective-permute-start.6) | collective-permute-done | bytes 24608 | tf_op jit(solution)/shard_map/ppermute | solution.py:331
  74.5 1.5 collective-permute-start.49
  76.7 1.1 slice_add_fusion.11
  77.8 3.4 %collective-permute-done.7 = f32[12,512]{1,0:T(8,128)S(1)} collective-permute-done((f32[12,512]{1,0:T(8,128)S(1)}, f32[12,512]{1,0:T(8,128)S(1)}, u32[]{:S(2)}, u32[]{:S(2)}) %collective-permute-start.7) | collective-permute-done | bytes 24608 | tf_op jit(solution)/shard_map/ppermute | solution.py:331
  82.9 2.6 %collective-permute-done.20.refs_6_ = f32[1,64,128]{2,1,0:T(8,128)S(1)} collective-permute-done((f32[1,64,128]{2,1,0:T(8,128)S(1)}, f32[1,64,128]{2,1,0:T(8,128)S(1)}, u32[]{:S(2)}, u32[]{:S(2)}) %collective-permute-start.20) | collective-permute-done | bytes 32800 | tf_op jit(solution)/shard_map/ppermute | solution.py:331
  85.9 2.9 %collective-permute-start.42 = (f32[2,160,128]{2,1,0:T(8,128)S(1)}, f32[2,160,128]{2,1,0:T(8,128)S(1)}, u32[]{:S(2)}, u32[]{:S(2)}) collective-permute-start(f32[2,160,128]{2,1,0:T(8,128)S(1)} %get-tuple-element.111), channel_id=1, source_target_pairs={{0,16},{2,18},{4,20},{6,22},{8,24},{10,26},{12,28},{14,30},{16,0},... | collective-permute-start | bytes 491528 | tf_op jit(solution)/shard_map/ppermute | solution.py:331
  88.8 1.8 collective-permute-start.34
  90.6 1.0 slice_add_fusion.21
  91.6 1.7 collective-permute-done.9
  94.3 3.6 %collective-permute-done.26 = f32[2,96,128]{2,1,0:T(8,128)S(1)} collective-permute-done((f32[2,96,128]{2,1,0:T(8,128)S(1)}, f32[2,96,128]{2,1,0:T(8,128)S(1)}, u32[]{:S(2)}, u32[]{:S(2)}) %collective-permute-start.26) | collective-permute-done | bytes 98336 | tf_op jit(solution)/shard_map/ppermute | solution.py:331
  97.9 1.1 collective-permute-start.22
  99.6 3.3 %collective-permute-done.22.refs_8_ = f32[4,64,128]{2,1,0:T(8,128)S(1)} collective-permute-done((f32[4,64,128]{2,1,0:T(8,128)S(1)}, f32[4,64,128]{2,1,0:T(8,128)S(1)}, u32[]{:S(2)}, u32[]{:S(2)}) %collective-permute-start.22) | collective-permute-done | bytes 131104 | tf_op jit(solution)/shard_map/ppermute | solution.py:331
  103.6 2.4 %collective-permute-done.27 = f32[1,96,128]{2,1,0:T(8,128)S(1)} collective-permute-done((f32[1,96,128]{2,1,0:T(8,128)S(1)}, f32[1,96,128]{2,1,0:T(8,128)S(1)}, u32[]{:S(2)}, u32[]{:S(2)}) %collective-permute-start.27) | collective-permute-done | bytes 49184 | tf_op jit(solution)/shard_map/ppermute | solution.py:331
  106.1 2.9 %collective-permute-done.11 = f32[1,96,128]{2,1,0:T(8,128)S(1)} collective-permute-done((f32[1,96,128]{2,1,0:T(8,128)S(1)}, f32[1,96,128]{2,1,0:T(8,128)S(1)}, u32[]{:S(2)}, u32[]{:S(2)}) %collective-permute-start.11) | collective-permute-done | bytes 49184 | tf_op jit(solution)/shard_map/ppermute | solution.py:331
  109.2 2.9 %collective-permute-start.12 = (f32[1,96,128]{2,1,0:T(8,128)S(1)}, f32[1,96,128]{2,1,0:T(8,128)S(1)}, u32[]{:S(2)}, u32[]{:S(2)}) collective-permute-start(f32[1,96,128]{2,1,0:T(8,128)S(1)} %fusion.8.refs_0_), channel_id=1, source_target_pairs={{0,16},{2,18},{4,20},{6,22},{8,24},{10,26},{12,28},{14,30},{16,0},... | collective-permute-start | bytes 147464 | tf_op jit(solution)/shard_map/ppermute | solution.py:331
  112.1 1.7 collective-permute-start.43
  113.9 1.1 slice_add_fusion.7
  115.0 2.4 %collective-permute-start.50 = (f32[2,192,128]{2,1,0:T(8,128)S(1)}, f32[2,192,128]{2,1,0:T(8,128)S(1)}, u32[]{:S(2)}, u32[]{:S(2)}) collective-permute-start(f32[2,192,128]{2,1,0:T(8,128)S(1)} %get-tuple-element.105), channel_id=1, source_target_pairs={{0,8},{2,10},{4,12},{6,14},{8,0},{10,2},{12,4},{14,6},{16,24},{18,... | collective-permute-start | bytes 589832 | tf_op jit(solution)/shard_map/ppermute | solution.py:331
  118.4 3.2 %collective-permute-done.35 = f32[1,160,128]{2,1,0:T(8,128)S(1)} collective-permute-done((f32[1,160,128]{2,1,0:T(8,128)S(1)}, f32[1,160,128]{2,1,0:T(8,128)S(1)}, u32[]{:S(2)}, u32[]{:S(2)}) %collective-permute-start.35) | collective-permute-done | bytes 81952 | tf_op jit(solution)/shard_map/ppermute | solution.py:331
  122.3 1.2 collective-permute-done.50
  124.6 2.0 %collective-permute-start.51 = (f32[1,192,128]{2,1,0:T(8,128)S(1)}, f32[1,192,128]{2,1,0:T(8,128)S(1)}, u32[]{:S(2)}, u32[]{:S(2)}) collective-permute-start(f32[1,192,128]{2,1,0:T(8,128)S(1)} %slice_add_fusion.18), channel_id=1, source_target_pairs={{0,16},{2,18},{4,20},{6,22},{8,24},{10,26},{12,28},{14,30},{16,0},... | collective-permute-start | bytes 294920 | tf_op jit(solution)/shard_map/ppermute | solution.py:331
  126.5 5.4 %collective-permute-done.51 = f32[1,192,128]{2,1,0:T(8,128)S(1)} collective-permute-done((f32[1,192,128]{2,1,0:T(8,128)S(1)}, f32[1,192,128]{2,1,0:T(8,128)S(1)}, u32[]{:S(2)}, u32[]{:S(2)}) %collective-permute-start.51) | collective-permute-done | bytes 98336 | tf_op jit(solution)/shard_map/ppermute | solution.py:331
  132.0 1.1 collective-permute-start.30
  133.2 5.8 %collective-permute-done.52.refs_11_ = f32[1,192,128]{2,1,0:T(8,128)S(1)} collective-permute-done((f32[1,192,128]{2,1,0:T(8,128)S(1)}, f32[1,192,128]{2,1,0:T(8,128)S(1)}, u32[]{:S(2)}, u32[]{:S(2)}) %collective-permute-start.52) | collective-permute-done | bytes 98336 | tf_op jit(solution)/shard_map/ppermute | solution.py:331
  139.1 2.3 %collective-permute-start.53 = (f32[2,192,128]{2,1,0:T(8,128)S(1)}, f32[2,192,128]{2,1,0:T(8,128)S(1)}, u32[]{:S(2)}, u32[]{:S(2)}) collective-permute-start(f32[2,192,128]{2,1,0:T(8,128)S(1)} %pad_maximum_fusion.12), channel_id=1, source_target_pairs={{0,8},{2,10},{4,12},{6,14},{8,0},{10,2},{12,4},{14,6},{16,24},{18,... | collective-permute-start | bytes 589832 | tf_op jit(solution)/shard_map/ppermute | solution.py:331
  141.4 4.7 %collective-permute-done.45.refs_7_ = f32[2,160,128]{2,1,0:T(8,128)S(1)} collective-permute-done((f32[2,160,128]{2,1,0:T(8,128)S(1)}, f32[2,160,128]{2,1,0:T(8,128)S(1)}, u32[]{:S(2)}, u32[]{:S(2)}) %collective-permute-start.45) | collective-permute-done | bytes 163872 | tf_op jit(solution)/shard_map/ppermute | solution.py:331
  146.1 1.1 collective-permute-start.37
  147.6 1.3 collective-permute-start.46
  149.0 1.3 collective-permute-start.54
  150.3 2.5 %collective-permute-done.37.refs_2_ = f32[2,160,128]{2,1,0:T(8,128)S(1)} collective-permute-done((f32[2,160,128]{2,1,0:T(8,128)S(1)}, f32[2,160,128]{2,1,0:T(8,128)S(1)}, u32[]{:S(2)}, u32[]{:S(2)}) %collective-permute-start.37) | collective-permute-done | bytes 163872 | tf_op jit(solution)/shard_map/ppermute | solution.py:331
  152.9 2.1 %collective-permute-start.38 = (f32[4,160,128]{2,1,0:T(8,128)S(1)}, f32[4,160,128]{2,1,0:T(8,128)S(1)}, u32[]{:S(2)}, u32[]{:S(2)}) collective-permute-start(f32[4,160,128]{2,1,0:T(8,128)S(1)} %pad_maximum_fusion.7), channel_id=1, source_target_pairs={{0,8},{2,10},{4,12},{6,14},{8,0},{10,2},{12,4},{14,6},{16,24},{18,... | collective-permute-start | bytes 983048 | tf_op jit(solution)/shard_map/ppermute | solution.py:331
  155.8 1.6 collective-permute-done.46.refs_8_
  157.4 2.2 %collective-permute-start.31 = (f32[8,96,128]{2,1,0:T(8,128)}, f32[8,96,128]{2,1,0:T(8,128)}, u32[]{:S(2)}, u32[]{:S(2)}) collective-permute-start(f32[8,96,128]{2,1,0:T(8,128)} %pad_maximum_fusion.5), channel_id=1, source_target_pairs={{0,2},{2,0},{4,6},{6,4},{8,10},{10,8},{12,14},{14,12},{16,18},{18,... | collective-permute-start | bytes 1179656 | tf_op jit(solution)/shard_map/ppermute | solution.py:331
  161.8 3.3 %collective-permute-done.38.refs_3_ = f32[4,160,128]{2,1,0:T(8,128)S(1)} collective-permute-done((f32[4,160,128]{2,1,0:T(8,128)S(1)}, f32[4,160,128]{2,1,0:T(8,128)S(1)}, u32[]{:S(2)}, u32[]{:S(2)}) %collective-permute-start.38) | collective-permute-done | bytes 327712 | tf_op jit(solution)/shard_map/ppermute | solution.py:331
  165.1 1.3 collective-permute-start.55
  167.2 1.5 collective-permute-start.39
  171.3 11.0 %collective-permute-done.15.refs_4_ = f32[8,96,128]{2,1,0:T(8,128)S(1)} collective-permute-done((f32[8,96,128]{2,1,0:T(8,128)S(1)}, f32[8,96,128]{2,1,0:T(8,128)S(1)}, u32[]{:S(2)}, u32[]{:S(2)}) %collective-permute-start.15) | collective-permute-done | bytes 393248 | tf_op jit(solution)/shard_map/ppermute | solution.py:331
  183.0 3.0 %collect_att.1 = (f32[512,256]{1,0:T(8,128)}, f32[512,256]{1,0:T(8,128)}, f32[512,256]{1,0:T(8,128)}, f32[256,512]{1,0:T(8,128)}) custom-call(s32[1]{0:T(128)} %bitcast.me_ref, f32[1,96,128]{2,1,0:T(8,128)} %copy-done.13, f32[1,96,128]{2,1,0:T(8,128)} %copy-done.22, f32[2,96,128]{2,1,0:T(8,128)} %copy-done.15, f32[4,96,128]{2,1,0:T(8,128)} %copy-done.19, ...), custom_call_target="tpu_custom_call" | custom-call | tf_op jit(solution)/shard_map/collect_att/pallas_call | solution.py:320
  186.1 2.6 %pad_maximum_fusion = f32[3,512,256]{2,1,0:T(8,128)} fusion(f32[1,512,256]{2,1,0:T(8,128)} %bitcast.24, f32[1,512,256]{2,1,0:T(8,128)} %bitcast.23, f32[1,512,256]{2,1,0:T(8,128)} %bitcast.22), kind=kLoop, calls=%fused_computation.2 | loop fusion | flops 786432 | bytes 3145728 | tf_op jit(solution)/shard_map/stack | solution.py:457
  190.4 4.6 %collect_mlp.1 = (f32[512,1024]{1,0:T(8,128)}, f32[1024,512]{1,0:T(8,128)}) custom-call(s32[1]{0:T(128)} %bitcast.me_ref, f32[1,160,128]{2,1,0:T(8,128)} %copy-done.2, f32[1,160,128]{2,1,0:T(8,128)} %copy-done.11, f32[2,160,128]{2,1,0:T(8,128)} %copy-done.7, f32[4,160,128]{2,1,0:T(8,128)} %copy-done.9, f32[8,160,128]{2,1,0:T(8,128)} %copy-done.23, ...), custom_call_target="tpu_custom_call" | custom-call | tf_op jit(solution)/shard_map/collect_mlp/pallas_call | solution.py:320
  (202 shorter events, 25.3 us)
Async XLA Ops:
  6.4 2.1 %collective-permute-start = (f32[196,512]{1,0:T(8,128)}, f32[196,512]{1,0:T(8,128)S(1)}, u32[]{:S(2)}, u32[]{:S(2)}) collective-permute-start(f32[196,512]{1,0:T(8,128)} %get-tuple-element.49.own_ref), channel_id=1, source_target_pairs={{0,1},{1,0},{2,3},{3,2},{4,5},{5,4},{6,7},{7,6},{8,9},{9,8},{10,11... | collective-permute-start | bytes 1204232 | tf_op jit(solution)/shard_map/ppermute | solution.py:335
  16.4 19.4 %collective-permute-start.40 = (f32[8,160,128]{2,1,0:T(8,128)}, f32[8,160,128]{2,1,0:T(8,128)}, u32[]{:S(2)}, u32[]{:S(2)}) collective-permute-start(f32[8,160,128]{2,1,0:T(8,128)} %get-tuple-element.78), channel_id=1, source_target_pairs={{0,8},{2,10},{4,12},{6,14},{8,0},{10,2},{12,4},{14,6},{16,24},{18,... | collective-permute-start | bytes 1966088 | tf_op jit(solution)/shard_map/ppermute | solution.py:331
  19.3 3.7 %collective-permute-start.1 = (f32[196,512]{1,0:T(8,128)}, f32[196,512]{1,0:T(8,128)S(1)}, u32[]{:S(2)}, u32[]{:S(2)}) collective-permute-start(f32[196,512]{1,0:T(8,128)} %get-tuple-element.50.own_ref), channel_id=1, source_target_pairs={{0,1},{1,0},{2,3},{3,2},{4,5},{5,4},{6,7},{7,6},{8,9},{9,8},{10,11... | collective-permute-start | bytes 1204232 | tf_op jit(solution)/shard_map/ppermute | solution.py:335
  19.3 3.7 %collective-permute-start.2 = (f32[196,512]{1,0:T(8,128)}, f32[196,512]{1,0:T(8,128)S(1)}, u32[]{:S(2)}, u32[]{:S(2)}) collective-permute-start(f32[196,512]{1,0:T(8,128)} %get-tuple-element.51.mown_ref), channel_id=1, source_target_pairs={{0,1},{1,0},{2,3},{3,2},{4,5},{5,4},{6,7},{7,6},{8,9},{9,8},{10,11... | collective-permute-start | bytes 1204232 | tf_op jit(solution)/shard_map/ppermute | solution.py:335
  20.0 42.0 %collective-permute-start.48 = (f32[8,192,128]{2,1,0:T(8,128)}, f32[8,192,128]{2,1,0:T(8,128)S(1)}, u32[]{:S(2)}, u32[]{:S(2)}) collective-permute-start(f32[8,192,128]{2,1,0:T(8,128)} %get-tuple-element.80), channel_id=1, source_target_pairs={{0,2},{2,0},{4,6},{6,4},{8,10},{10,8},{12,14},{14,12},{16,18},{18,... | collective-permute-start | bytes 2359304 | tf_op jit(solution)/shard_map/ppermute | solution.py:331
  21.5 18.7 %collective-permute-start.32 = (f32[8,160,128]{2,1,0:T(8,128)}, f32[8,160,128]{2,1,0:T(8,128)}, u32[]{:S(2)}, u32[]{:S(2)}) collective-permute-start(f32[8,160,128]{2,1,0:T(8,128)} %get-tuple-element.76), channel_id=1, source_target_pairs={{0,4},{2,6},{4,0},{6,2},{8,12},{10,14},{12,8},{14,10},{16,20},{18,... | collective-permute-start | bytes 1966088 | tf_op jit(solution)/shard_map/ppermute | solution.py:331
  31.6 36.5 %collective-permute-start.24 = (f32[8,96,128]{2,1,0:T(8,128)}, f32[8,96,128]{2,1,0:T(8,128)}, u32[]{:S(2)}, u32[]{:S(2)}) collective-permute-start(f32[8,96,128]{2,1,0:T(8,128)} %get-tuple-element.70), channel_id=1, source_target_pairs={{0,2},{2,0},{4,6},{6,4},{8,10},{10,8},{12,14},{14,12},{16,18},{18,... | collective-permute-start | bytes 1179656 | tf_op jit(solution)/shard_map/ppermute | solution.py:331
  32.2 8.0 %collective-permute-start.16 = (f32[8,64,128]{2,1,0:T(8,128)}, f32[8,64,128]{2,1,0:T(8,128)S(1)}, u32[]{:S(2)}, u32[]{:S(2)}) collective-permute-start(f32[8,64,128]{2,1,0:T(8,128)} %get-tuple-element.68), channel_id=1, source_target_pairs={{0,8},{2,10},{4,12},{6,14},{8,0},{10,2},{12,4},{14,6},{16,24},{18,... | collective-permute-start | bytes 786440 | tf_op jit(solution)/shard_map/ppermute | solution.py:331
  35.8 40.4 %collective-permute-start.8 = (f32[8,96,128]{2,1,0:T(8,128)}, f32[8,96,128]{2,1,0:T(8,128)}, u32[]{:S(2)}, u32[]{:S(2)}) collective-permute-start(f32[8,96,128]{2,1,0:T(8,128)} %get-tuple-element.66), channel_id=1, source_target_pairs={{0,4},{2,6},{4,0},{6,2},{8,12},{10,14},{12,8},{14,10},{16,20},{18,... | collective-permute-start | bytes 1179656 | tf_op jit(solution)/shard_map/ppermute | solution.py:331
  40.2 3.7 %collective-permute-start.3 = (f32[196,512]{1,0:T(8,128)}, f32[196,512]{1,0:T(8,128)}, u32[]{:S(2)}, u32[]{:S(2)}) collective-permute-start(f32[196,512]{1,0:T(8,128)} %get-tuple-element.58.own_ref), channel_id=1, source_target_pairs={{0,1},{1,0},{2,3},{3,2},{4,5},{5,4},{6,7},{7,6},{8,9},{9,8},{10,11... | collective-permute-start | bytes 1204232 | tf_op jit(solution)/shard_map/ppermute | solution.py:335
  40.3 11.6 %collective-permute-start.17 = (f32[4,64,128]{2,1,0:T(8,128)S(1)}, f32[4,64,128]{2,1,0:T(8,128)S(1)}, u32[]{:S(2)}, u32[]{:S(2)}) collective-permute-start(f32[4,64,128]{2,1,0:T(8,128)S(1)} %get-tuple-element.115), channel_id=1, source_target_pairs={{0,2},{2,0},{4,6},{6,4},{8,10},{10,8},{12,14},{14,12},{16,18},{18,... | collective-permute-start | bytes 393224 | tf_op jit(solution)/shard_map/ppermute | solution.py:331
  43.9 41.7 %collective-permute-start.41 = (f32[4,160,128]{2,1,0:T(8,128)}, f32[4,160,128]{2,1,0:T(8,128)S(1)}, u32[]{:S(2)}, u32[]{:S(2)}) collective-permute-start(f32[4,160,128]{2,1,0:T(8,128)} %get-tuple-element.101), channel_id=1, source_target_pairs={{0,2},{2,0},{4,6},{6,4},{8,10},{10,8},{12,14},{14,12},{16,18},{18,... | collective-permute-start | bytes 983048 | tf_op jit(solution)/shard_map/ppermute | solution.py:331
  51.9 6.8 %collective-permute-start.4 = (f32[12,512]{1,0:T(8,128)S(1)}, f32[12,512]{1,0:T(8,128)S(1)}, u32[]{:S(2)}, u32[]{:S(2)}) collective-permute-start(f32[12,512]{1,0:T(8,128)S(1)} %pad_maximum_fusion.19), channel_id=1, source_target_pairs={{0,2},{2,0},{4,6},{6,4},{8,10},{10,8},{12,14},{14,12},{16,18},{18,... | collective-permute-start | bytes 73736 | tf_op jit(solution)/shard_map/ppermute | solution.py:331
  58.7 7.8 %collective-permute-start.18 = (f32[2,64,128]{2,1,0:T(8,128)S(1)}, f32[2,64,128]{2,1,0:T(8,128)S(1)}, u32[]{:S(2)}, u32[]{:S(2)}) collective-permute-start(f32[2,64,128]{2,1,0:T(8,128)S(1)} %get-tuple-element.121), channel_id=1, source_target_pairs={{0,16},{2,18},{4,20},{6,22},{8,24},{10,26},{12,28},{14,30},{16,0},... | collective-permute-start | bytes 196616 | tf_op jit(solution)/shard_map/ppermute | solution.py:331
  62.0 4.0 %collective-permute-start.5 = (f32[12,512]{1,0:T(8,128)S(1)}, f32[12,512]{1,0:T(8,128)S(1)}, u32[]{:S(2)}, u32[]{:S(2)}) collective-permute-start(f32[12,512]{1,0:T(8,128)S(1)} %fusion.10), channel_id=1, source_target_pairs={{0,4},{2,6},{4,0},{6,2},{8,12},{10,14},{12,8},{14,10},{16,20},{18,... | collective-permute-start | bytes 73736 | tf_op jit(solution)/shard_map/ppermute | solution.py:331
  66.0 20.0 %collective-permute-start.33 = (f32[4,160,128]{2,1,0:T(8,128)}, f32[4,160,128]{2,1,0:T(8,128)S(1)}, u32[]{:S(2)}, u32[]{:S(2)}) collective-permute-start(f32[4,160,128]{2,1,0:T(8,128)} %get-tuple-element.103), channel_id=1, source_target_pairs={{0,8},{2,10},{4,12},{6,14},{8,0},{10,2},{12,4},{14,6},{16,24},{18,... | collective-permute-start | bytes 983048 | tf_op jit(solution)/shard_map/ppermute | solution.py:331
  66.4 8.1 %collective-permute-start.6 = (f32[12,512]{1,0:T(8,128)S(1)}, f32[12,512]{1,0:T(8,128)S(1)}, u32[]{:S(2)}, u32[]{:S(2)}) collective-permute-start(f32[12,512]{1,0:T(8,128)S(1)} %add.141), channel_id=1, source_target_pairs={{0,8},{2,10},{4,12},{6,14},{8,0},{10,2},{12,4},{14,6},{16,24},{18,... | collective-permute-start | bytes 73736 | tf_op jit(solution)/shard_map/ppermute | solution.py:331
  68.1 7.9 %collective-permute-start.19 = (f32[1,64,128]{2,1,0:T(8,128)S(1)}, f32[1,64,128]{2,1,0:T(8,128)S(1)}, u32[]{:S(2)}, u32[]{:S(2)}) collective-permute-start(f32[1,64,128]{2,1,0:T(8,128)S(1)} %slice_add_fusion.34), channel_id=1, source_target_pairs={{0,4},{2,6},{4,0},{6,2},{8,12},{10,14},{12,8},{14,10},{16,20},{18,... | collective-permute-start | bytes 98312 | tf_op jit(solution)/shard_map/ppermute | solution.py:331
  74.5 39.3 %collective-permute-start.49 = (f32[4,192,128]{2,1,0:T(8,128)S(1)}, f32[4,192,128]{2,1,0:T(8,128)}, u32[]{:S(2)}, u32[]{:S(2)}) collective-permute-start(f32[4,192,128]{2,1,0:T(8,128)S(1)} %get-tuple-element.99), channel_id=1, source_target_pairs={{0,4},{2,6},{4,0},{6,2},{8,12},{10,14},{12,8},{14,10},{16,20},{18,... | collective-permute-start | bytes 1179656 | tf_op jit(solution)/shard_map/ppermute | solution.py:331
  76.0 5.2 %collective-permute-start.7 = (f32[12,512]{1,0:T(8,128)S(1)}, f32[12,512]{1,0:T(8,128)S(1)}, u32[]{:S(2)}, u32[]{:S(2)}) collective-permute-start(f32[12,512]{1,0:T(8,128)S(1)} %add.142), channel_id=1, source_target_pairs={{0,16},{2,18},{4,20},{6,22},{8,24},{10,26},{12,28},{14,30},{16,0},... | collective-permute-start | bytes 73736 | tf_op jit(solution)/shard_map/ppermute | solution.py:331
  76.1 9.3 %collective-permute-start.20 = (f32[1,64,128]{2,1,0:T(8,128)S(1)}, f32[1,64,128]{2,1,0:T(8,128)S(1)}, u32[]{:S(2)}, u32[]{:S(2)}) collective-permute-start(f32[1,64,128]{2,1,0:T(8,128)S(1)} %fusion.9.refs_5_), channel_id=1, source_target_pairs={{0,4},{2,6},{4,0},{6,2},{8,12},{10,14},{12,8},{14,10},{16,20},{18,... | collective-permute-start | bytes 98312 | tf_op jit(solution)/shard_map/ppermute | solution.py:331
  81.2 7.6 %collective-permute-start.25 = (f32[4,96,128]{2,1,0:T(8,128)S(1)}, f32[4,96,128]{2,1,0:T(8,128)}, u32[]{:S(2)}, u32[]{:S(2)}) collective-permute-start(f32[4,96,128]{2,1,0:T(8,128)S(1)} %get-tuple-element.107), channel_id=1, source_target_pairs={{0,4},{2,6},{4,0},{6,2},{8,12},{10,14},{12,8},{14,10},{16,20},{18,... | collective-permute-start | bytes 589832 | tf_op jit(solution)/shard_map/ppermute | solution.py:331
  85.5 7.8 %collective-permute-start.9 = (f32[4,96,128]{2,1,0:T(8,128)S(1)}, f32[4,96,128]{2,1,0:T(8,128)S(1)}, u32[]{:S(2)}, u32[]{:S(2)}) collective-permute-start(f32[4,96,128]{2,1,0:T(8,128)S(1)} %get-tuple-element.109), channel_id=1, source_target_pairs={{0,8},{2,10},{4,12},{6,14},{8,0},{10,2},{12,4},{14,6},{16,24},{18,... | collective-permute-start | bytes 589832 | tf_op jit(solution)/shard_map/ppermute | solution.py:331
  85.7 7.7 %collective-permute-start.21 = (f32[2,64,128]{2,1,0:T(8,128)S(1)}, f32[2,64,128]{2,1,0:T(8,128)S(1)}, u32[]{:S(2)}, u32[]{:S(2)}) collective-permute-start(f32[2,64,128]{2,1,0:T(8,128)S(1)} %pad_maximum_fusion.18), channel_id=1, source_target_pairs={{0,16},{2,18},{4,20},{6,22},{8,24},{10,26},{12,28},{14,30},{16,0},... | collective-permute-start | bytes 196616 | tf_op jit(solution)/shard_map/ppermute | solution.py:331
  85.9 23.2 %collective-permute-start.42 = (f32[2,160,128]{2,1,0:T(8,128)S(1)}, f32[2,160,128]{2,1,0:T(8,128)S(1)}, u32[]{:S(2)}, u32[]{:S(2)}) collective-permute-start(f32[2,160,128]{2,1,0:T(8,128)S(1)} %get-tuple-element.111), channel_id=1, source_target_pairs={{0,16},{2,18},{4,20},{6,22},{8,24},{10,26},{12,28},{14,30},{16,0},... | collective-permute-start | bytes 491528 | tf_op jit(solution)/shard_map/ppermute | solution.py:331
  88.8 23.3 %collective-permute-start.34 = (f32[2,160,128]{2,1,0:T(8,128)S(1)}, f32[2,160,128]{2,1,0:T(8,128)S(1)}, u32[]{:S(2)}, u32[]{:S(2)}) collective-permute-start(f32[2,160,128]{2,1,0:T(8,128)S(1)} %get-tuple-element.113), channel_id=1, source_target_pairs={{0,2},{2,0},{4,6},{6,4},{8,10},{10,8},{12,14},{14,12},{16,18},{18,... | collective-permute-start | bytes 491528 | tf_op jit(solution)/shard_map/ppermute | solution.py:331
  93.3 4.6 %collective-permute-start.26 = (f32[2,96,128]{2,1,0:T(8,128)S(1)}, f32[2,96,128]{2,1,0:T(8,128)S(1)}, u32[]{:S(2)}, u32[]{:S(2)}) collective-permute-start(f32[2,96,128]{2,1,0:T(8,128)S(1)} %get-tuple-element.117), channel_id=1, source_target_pairs={{0,8},{2,10},{4,12},{6,14},{8,0},{10,2},{12,4},{14,6},{16,24},{18,... | collective-permute-start | bytes 294920 | tf_op jit(solution)/shard_map/ppermute | solution.py:331
  93.4 5.7 %collective-permute-start.10 = (f32[2,96,128]{2,1,0:T(8,128)S(1)}, f32[2,96,128]{2,1,0:T(8,128)S(1)}, u32[]{:S(2)}, u32[]{:S(2)}) collective-permute-start(f32[2,96,128]{2,1,0:T(8,128)S(1)} %get-tuple-element.119), channel_id=1, source_target_pairs={{0,2},{2,0},{4,6},{6,4},{8,10},{10,8},{12,14},{14,12},{16,18},{18,... | collective-permute-start | bytes 294920 | tf_op jit(solution)/shard_map/ppermute | solution.py:331
  97.9 5.0 %collective-permute-start.22 = (f32[4,64,128]{2,1,0:T(8,128)S(1)}, f32[4,64,128]{2,1,0:T(8,128)S(1)}, u32[]{:S(2)}, u32[]{:S(2)}) collective-permute-start(f32[4,64,128]{2,1,0:T(8,128)S(1)} %pad_maximum_fusion.15), channel_id=1, source_target_pairs={{0,2},{2,0},{4,6},{6,4},{8,10},{10,8},{12,14},{14,12},{16,18},{18,... | collective-permute-start | bytes 393224 | tf_op jit(solution)/shard_map/ppermute | solution.py:331
  99.1 6.9 %collective-permute-start.27 = (f32[1,96,128]{2,1,0:T(8,128)S(1)}, f32[1,96,128]{2,1,0:T(8,128)S(1)}, u32[]{:S(2)}, u32[]{:S(2)}) collective-permute-start(f32[1,96,128]{2,1,0:T(8,128)S(1)} %slice_add_fusion.30), channel_id=1, source_target_pairs={{0,16},{2,18},{4,20},{6,22},{8,24},{10,26},{12,28},{14,30},{16,0},... | collective-permute-start | bytes 147464 | tf_op jit(solution)/shard_map/ppermute | solution.py:331
  102.9 6.2 %collective-permute-start.11 = (f32[1,96,128]{2,1,0:T(8,128)S(1)}, f32[1,96,128]{2,1,0:T(8,128)S(1)}, u32[]{:S(2)}, u32[]{:S(2)}) collective-permute-start(f32[1,96,128]{2,1,0:T(8,128)S(1)} %slice_add_fusion.32), channel_id=1, source_target_pairs={{0,16},{2,18},{4,20},{6,22},{8,24},{10,26},{12,28},{14,30},{16,0},... | collective-permute-start | bytes 147464 | tf_op jit(solution)/shard_map/ppermute | solution.py:331
  106.0 62.8 %collective-permute-start.23 = (f32[8,64,128]{2,1,0:T(8,128)S(1)}, f32[8,64,128]{2,1,0:T(8,128)S(1)}, u32[]{:S(2)}, u32[]{:S(2)}) collective-permute-start(f32[8,64,128]{2,1,0:T(8,128)S(1)} %pad_maximum_fusion.9), channel_id=1, source_target_pairs={{0,8},{2,10},{4,12},{6,14},{8,0},{10,2},{12,4},{14,6},{16,24},{18,... | collective-permute-start | bytes 786440 | tf_op jit(solution)/shard_map/ppermute | solution.py:331
  106.1 48.8 %copy-start.12 = (f32[1,96,128]{2,1,0:T(8,128)}, f32[1,96,128]{2,1,0:T(8,128)S(1)}, u32[]{:S(2)}) copy-start(f32[1,96,128]{2,1,0:T(8,128)S(1)} %fusion.7.refs_10_) | copy-start | bytes 147460
  109.1 5.9 %collective-permute-start.28 = (f32[1,96,128]{2,1,0:T(8,128)S(1)}, f32[1,96,128]{2,1,0:T(8,128)S(1)}, u32[]{:S(2)}, u32[]{:S(2)}) collective-permute-start(f32[1,96,128]{2,1,0:T(8,128)S(1)} %fusion.7.refs_10_), channel_id=1, source_target_pairs={{0,16},{2,18},{4,20},{6,22},{8,24},{10,26},{12,28},{14,30},{16,0},... | collective-permute-start | bytes 147464 | tf_op jit(solution)/shard_map/ppermute | solution.py:331
  109.2 59.6 %copy-start.13 = (f32[1,96,128]{2,1,0:T(8,128)}, f32[1,96,128]{2,1,0:T(8,128)S(1)}, u32[]{:S(2)}) copy-start(f32[1,96,128]{2,1,0:T(8,128)S(1)} %fusion.8.refs_0_) | copy-start | bytes 147460
  109.2 8.3 %collective-permute-start.12 = (f32[1,96,128]{2,1,0:T(8,128)S(1)}, f32[1,96,128]{2,1,0:T(8,128)S(1)}, u32[]{:S(2)}, u32[]{:S(2)}) collective-permute-start(f32[1,96,128]{2,1,0:T(8,128)S(1)} %fusion.8.refs_0_), channel_id=1, source_target_pairs={{0,16},{2,18},{4,20},{6,22},{8,24},{10,26},{12,28},{14,30},{16,0},... | collective-permute-start | bytes 147464 | tf_op jit(solution)/shard_map/ppermute | solution.py:331
  112.1 5.4 %collective-permute-start.43 = (f32[1,160,128]{2,1,0:T(8,128)S(1)}, f32[1,160,128]{2,1,0:T(8,128)S(1)}, u32[]{:S(2)}, u32[]{:S(2)}) collective-permute-start(f32[1,160,128]{2,1,0:T(8,128)S(1)} %slice_add_fusion.24), channel_id=1, source_target_pairs={{0,4},{2,6},{4,0},{6,2},{8,12},{10,14},{12,8},{14,10},{16,20},{18,... | collective-permute-start | bytes 245768 | tf_op jit(solution)/shard_map/ppermute | solution.py:331
  113.8 7.7 %collective-permute-start.35 = (f32[1,160,128]{2,1,0:T(8,128)S(1)}, f32[1,160,128]{2,1,0:T(8,128)S(1)}, u32[]{:S(2)}, u32[]{:S(2)}) collective-permute-start(f32[1,160,128]{2,1,0:T(8,128)S(1)} %slice_add_fusion.26), channel_id=1, source_target_pairs={{0,16},{2,18},{4,20},{6,22},{8,24},{10,26},{12,28},{14,30},{16,0},... | collective-permute-start | bytes 245768 | tf_op jit(solution)/shard_map/ppermute | solution.py:331
  115.0 40.0 %copy-start.21 = (f32[1,96,128]{2,1,0:T(8,128)}, f32[1,96,128]{2,1,0:T(8,128)S(1)}, u32[]{:S(2)}) copy-start(f32[1,96,128]{2,1,0:T(8,128)S(1)} %collective-permute-done.28.refs_11_) | copy-start | bytes 147460
  115.0 8.5 %collective-permute-start.50 = (f32[2,192,128]{2,1,0:T(8,128)S(1)}, f32[2,192,128]{2,1,0:T(8,128)S(1)}, u32[]{:S(2)}, u32[]{:S(2)}) collective-permute-start(f32[2,192,128]{2,1,0:T(8,128)S(1)} %get-tuple-element.105), channel_id=1, source_target_pairs={{0,8},{2,10},{4,12},{6,14},{8,0},{10,2},{12,4},{14,6},{16,24},{18,... | collective-permute-start | bytes 589832 | tf_op jit(solution)/shard_map/ppermute | solution.py:331
  117.4 51.3 %copy-start.22 = (f32[1,96,128]{2,1,0:T(8,128)}, f32[1,96,128]{2,1,0:T(8,128)S(1)}, u32[]{:S(2)}) copy-start(f32[1,96,128]{2,1,0:T(8,128)S(1)} %collective-permute-done.12.refs_1_) | copy-start | bytes 147460
  117.4 7.1 %collective-permute-start.29 = (f32[2,96,128]{2,1,0:T(8,128)S(1)}, f32[2,96,128]{2,1,0:T(8,128)S(1)}, u32[]{:S(2)}, u32[]{:S(2)}) collective-permute-start(f32[2,96,128]{2,1,0:T(8,128)S(1)} %pad_maximum_fusion.17), channel_id=1, source_target_pairs={{0,8},{2,10},{4,12},{6,14},{8,0},{10,2},{12,4},{14,6},{16,24},{18,... | collective-permute-start | bytes 294920 | tf_op jit(solution)/shard_map/ppermute | solution.py:331
  117.6 31.4 %collective-permute-start.13 = (f32[2,96,128]{2,1,0:T(8,128)S(1)}, f32[2,96,128]{2,1,0:T(8,128)S(1)}, u32[]{:S(2)}, u32[]{:S(2)}) collective-permute-start(f32[2,96,128]{2,1,0:T(8,128)S(1)} %pad_maximum_fusion.16), channel_id=1, source_target_pairs={{0,2},{2,0},{4,6},{6,4},{8,10},{10,8},{12,14},{14,12},{16,18},{18,... | collective-permute-start | bytes 294920 | tf_op jit(solution)/shard_map/ppermute | solution.py:331
  118.3 41.2 %copy-start.1 = (f32[1,160,128]{2,1,0:T(8,128)}, f32[1,160,128]{2,1,0:T(8,128)S(1)}, u32[]{:S(2)}) copy-start(f32[1,160,128]{2,1,0:T(8,128)S(1)} %fusion.5.refs_5_) | copy-start | bytes 245764
  121.6 11.5 %collective-permute-start.44 = (f32[1,160,128]{2,1,0:T(8,128)S(1)}, f32[1,160,128]{2,1,0:T(8,128)S(1)}, u32[]{:S(2)}, u32[]{:S(2)}) collective-permute-start(f32[1,160,128]{2,1,0:T(8,128)S(1)} %fusion.5.refs_5_), channel_id=1, source_target_pairs={{0,4},{2,6},{4,0},{6,2},{8,12},{10,14},{12,8},{14,10},{16,20},{18,... | collective-permute-start | bytes 245768 | tf_op jit(solution)/shard_map/ppermute | solution.py:331
  122.3 44.0 %copy-start.2 = (f32[1,160,128]{2,1,0:T(8,128)}, f32[1,160,128]{2,1,0:T(8,128)S(1)}, u32[]{:S(2)}) copy-start(f32[1,160,128]{2,1,0:T(8,128)S(1)} %fusion.6.refs_0_) | copy-start | bytes 245764
  123.5 15.6 %collective-permute-start.36 = (f32[1,160,128]{2,1,0:T(8,128)S(1)}, f32[1,160,128]{2,1,0:T(8,128)S(1)}, u32[]{:S(2)}, u32[]{:S(2)}) collective-permute-start(f32[1,160,128]{2,1,0:T(8,128)S(1)} %fusion.6.refs_0_), channel_id=1, source_target_pairs={{0,16},{2,18},{4,20},{6,22},{8,24},{10,26},{12,28},{14,30},{16,0},... | collective-permute-start | bytes 245768 | tf_op jit(solution)/shard_map/ppermute | solution.py:331
  124.6 30.4 %copy-start.14 = (f32[2,96,128]{2,1,0:T(8,128)}, f32[2,96,128]{2,1,0:T(8,128)S(1)}, u32[]{:S(2)}) copy-start(f32[2,96,128]{2,1,0:T(8,128)S(1)} %collective-permute-done.29.refs_12_) | copy-start | bytes 294916
  124.6 7.4 %collective-permute-start.51 = (f32[1,192,128]{2,1,0:T(8,128)S(1)}, f32[1,192,128]{2,1,0:T(8,128)S(1)}, u32[]{:S(2)}, u32[]{:S(2)}) collective-permute-start(f32[1,192,128]{2,1,0:T(8,128)S(1)} %slice_add_fusion.18), channel_id=1, source_target_pairs={{0,16},{2,18},{4,20},{6,22},{8,24},{10,26},{12,28},{14,30},{16,0},... | collective-permute-start | bytes 294920 | tf_op jit(solution)/shard_map/ppermute | solution.py:331
  132.0 20.9 %collective-permute-start.30 = (f32[4,96,128]{2,1,0:T(8,128)S(1)}, f32[4,96,128]{2,1,0:T(8,128)S(1)}, u32[]{:S(2)}, u32[]{:S(2)}) collective-permute-start(f32[4,96,128]{2,1,0:T(8,128)S(1)} %pad_maximum_fusion.11), channel_id=1, source_target_pairs={{0,4},{2,6},{4,0},{6,2},{8,12},{10,14},{12,8},{14,10},{16,20},{18,... | collective-permute-start | bytes 589832 | tf_op jit(solution)/shard_map/ppermute | solution.py:331
  133.1 27.7 %copy-start = (f32[1,192,128]{2,1,0:T(8,128)}, f32[1,192,128]{2,1,0:T(8,128)S(1)}, u32[]{:S(2)}) copy-start(f32[1,192,128]{2,1,0:T(8,128)S(1)} %fusion.4.refs_10_) | copy-start | bytes 294916
  133.1 5.9 %collective-permute-start.52 = (f32[1,192,128]{2,1,0:T(8,128)S(1)}, f32[1,192,128]{2,1,0:T(8,128)S(1)}, u32[]{:S(2)}, u32[]{:S(2)}) collective-permute-start(f32[1,192,128]{2,1,0:T(8,128)S(1)} %fusion.4.refs_10_), channel_id=1, source_target_pairs={{0,16},{2,18},{4,20},{6,22},{8,24},{10,26},{12,28},{14,30},{16,0},... | collective-permute-start | bytes 294920 | tf_op jit(solution)/shard_map/ppermute | solution.py:331
  139.1 7.1 %collective-permute-start.45 = (f32[2,160,128]{2,1,0:T(8,128)S(1)}, f32[2,160,128]{2,1,0:T(8,128)S(1)}, u32[]{:S(2)}, u32[]{:S(2)}) collective-permute-start(f32[2,160,128]{2,1,0:T(8,128)S(1)} %pad_maximum_fusion.14), channel_id=1, source_target_pairs={{0,16},{2,18},{4,20},{6,22},{8,24},{10,26},{12,28},{14,30},{16,0},... | collective-permute-start | bytes 491528 | tf_op jit(solution)/shard_map/ppermute | solution.py:331
  139.1 8.5 %collective-permute-start.53 = (f32[2,192,128]{2,1,0:T(8,128)S(1)}, f32[2,192,128]{2,1,0:T(8,128)S(1)}, u32[]{:S(2)}, u32[]{:S(2)}) collective-permute-start(f32[2,192,128]{2,1,0:T(8,128)S(1)} %pad_maximum_fusion.12), channel_id=1, source_target_pairs={{0,8},{2,10},{4,12},{6,14},{8,0},{10,2},{12,4},{14,6},{16,24},{18,... | collective-permute-start | bytes 589832 | tf_op jit(solution)/shard_map/ppermute | solution.py:331
  146.1 6.7 %collective-permute-start.37 = (f32[2,160,128]{2,1,0:T(8,128)S(1)}, f32[2,160,128]{2,1,0:T(8,128)S(1)}, u32[]{:S(2)}, u32[]{:S(2)}) collective-permute-start(f32[2,160,128]{2,1,0:T(8,128)S(1)} %pad_maximum_fusion.13), channel_id=1, source_target_pairs={{0,2},{2,0},{4,6},{6,4},{8,10},{10,8},{12,14},{14,12},{16,18},{18,... | collective-permute-start | bytes 491528 | tf_op jit(solution)/shard_map/ppermute | solution.py:331
  147.6 9.7 %collective-permute-start.46 = (f32[4,160,128]{2,1,0:T(8,128)S(1)}, f32[4,160,128]{2,1,0:T(8,128)S(1)}, u32[]{:S(2)}, u32[]{:S(2)}) collective-permute-start(f32[4,160,128]{2,1,0:T(8,128)S(1)} %pad_maximum_fusion.8), channel_id=1, source_target_pairs={{0,2},{2,0},{4,6},{6,4},{8,10},{10,8},{12,14},{14,12},{16,18},{18,... | collective-permute-start | bytes 983048 | tf_op jit(solution)/shard_map/ppermute | solution.py:331
  149.0 11.5 %collective-permute-start.54 = (f32[4,192,128]{2,1,0:T(8,128)S(1)}, f32[4,192,128]{2,1,0:T(8,128)S(1)}, u32[]{:S(2)}, u32[]{:S(2)}) collective-permute-start(f32[4,192,128]{2,1,0:T(8,128)S(1)} %pad_maximum_fusion.6), channel_id=1, source_target_pairs={{0,4},{2,6},{4,0},{6,2},{8,12},{10,14},{12,8},{14,10},{16,20},{18,... | collective-permute-start | bytes 1179656 | tf_op jit(solution)/shard_map/ppermute | solution.py:331
  152.8 14.4 %collective-permute-start.14 = (f32[4,96,128]{2,1,0:T(8,128)S(1)}, f32[4,96,128]{2,1,0:T(8,128)S(1)}, u32[]{:S(2)}, u32[]{:S(2)}) collective-permute-start(f32[4,96,128]{2,1,0:T(8,128)S(1)} %pad_maximum_fusion.10), channel_id=1, source_target_pairs={{0,8},{2,10},{4,12},{6,14},{8,0},{10,2},{12,4},{14,6},{16,24},{18,... | collective-permute-start | bytes 589832 | tf_op jit(solution)/shard_map/ppermute | solution.py:331
  152.9 12.2 %collective-permute-start.38 = (f32[4,160,128]{2,1,0:T(8,128)S(1)}, f32[4,160,128]{2,1,0:T(8,128)S(1)}, u32[]{:S(2)}, u32[]{:S(2)}) collective-permute-start(f32[4,160,128]{2,1,0:T(8,128)S(1)} %pad_maximum_fusion.7), channel_id=1, source_target_pairs={{0,8},{2,10},{4,12},{6,14},{8,0},{10,2},{12,4},{14,6},{16,24},{18,... | collective-permute-start | bytes 983048 | tf_op jit(solution)/shard_map/ppermute | solution.py:331
  157.4 14.0 %collective-permute-start.31 = (f32[8,96,128]{2,1,0:T(8,128)}, f32[8,96,128]{2,1,0:T(8,128)}, u32[]{:S(2)}, u32[]{:S(2)}) collective-permute-start(f32[8,96,128]{2,1,0:T(8,128)} %pad_maximum_fusion.5), channel_id=1, source_target_pairs={{0,2},{2,0},{4,6},{6,4},{8,10},{10,8},{12,14},{14,12},{16,18},{18,... | collective-permute-start | bytes 1179656 | tf_op jit(solution)/shard_map/ppermute | solution.py:331
  160.4 28.2 %collective-permute-start.47 = (f32[8,160,128]{2,1,0:T(8,128)}, f32[8,160,128]{2,1,0:T(8,128)}, u32[]{:S(2)}, u32[]{:S(2)}) collective-permute-start(f32[8,160,128]{2,1,0:T(8,128)} %pad_maximum_fusion.3), channel_id=1, source_target_pairs={{0,8},{2,10},{4,12},{6,14},{8,0},{10,2},{12,4},{14,6},{16,24},{18,... | collective-permute-start | bytes 1966088 | tf_op jit(solution)/shard_map/ppermute | solution.py:331
  165.1 23.6 %collective-permute-start.55 = (f32[8,192,128]{2,1,0:T(8,128)}, f32[8,192,128]{2,1,0:T(8,128)S(1)}, u32[]{:S(2)}, u32[]{:S(2)}) collective-permute-start(f32[8,192,128]{2,1,0:T(8,128)} %pad_maximum_fusion.1), channel_id=1, source_target_pairs={{0,2},{2,0},{4,6},{6,4},{8,10},{10,8},{12,14},{14,12},{16,18},{18,... | collective-permute-start | bytes 2359304 | tf_op jit(solution)/shard_map/ppermute | solution.py:331
  167.2 21.5 %collective-permute-start.39 = (f32[8,160,128]{2,1,0:T(8,128)}, f32[8,160,128]{2,1,0:T(8,128)S(1)}, u32[]{:S(2)}, u32[]{:S(2)}) collective-permute-start(f32[8,160,128]{2,1,0:T(8,128)} %pad_maximum_fusion.2), channel_id=1, source_target_pairs={{0,4},{2,6},{4,0},{6,2},{8,12},{10,14},{12,8},{14,10},{16,20},{18,... | collective-permute-start | bytes 1966088 | tf_op jit(solution)/shard_map/ppermute | solution.py:331
  168.8 13.5 %collective-permute-start.15 = (f32[8,96,128]{2,1,0:T(8,128)S(1)}, f32[8,96,128]{2,1,0:T(8,128)S(1)}, u32[]{:S(2)}, u32[]{:S(2)}) collective-permute-start(f32[8,96,128]{2,1,0:T(8,128)S(1)} %pad_maximum_fusion.4), channel_id=1, source_target_pairs={{0,4},{2,6},{4,0},{6,2},{8,12},{10,14},{12,8},{14,10},{16,20},{18,... | collective-permute-start | bytes 1179656 | tf_op jit(solution)/shard_map/ppermute | solution.py:331
  (34 other events, 378.9 us)
